TPU v7x, 32 devices: a whole 2x2x4 slice. The times are simulated.
32 devices in a mesh: dp: 16 (over z, y, x), mp: 2 (over core).
Axes of the slice: x: 2, y: 2, z: 4, core: 2. Of those that a mesh axis runs over, the one named last changes fastest.
Arguments:
- tokens: bfloat16 [8192, 768], P('dp'), may hold values from -6 to 6
- lengths: int32 [16], P('dp'), may hold values from 40 to 512, as said below
- cotangent: bfloat16 [8192, 768], P('dp'), may hold values from -6 to 6
- query_weight: bfloat16 [768, 768], P(None, 'mp'), may hold values from -0.21875 to 0.21875
- query_bias: bfloat16 [768], P('mp'), may hold values from -3 to 3
- key_weight: bfloat16 [768, 768], P(None, 'mp'), may hold values from -0.21875 to 0.21875
- value_weight: bfloat16 [768, 768], P(None, 'mp'), may hold values from -0.21875 to 0.21875
- value_bias: bfloat16 [768], P('mp'), may hold values from -1 to 1
- out_weight: bfloat16 [768, 768], P('mp'), may hold values from -1.75 to 1.75
- out_bias: bfloat16 [768], replicated, may hold values from -3 to 3
- mid_gain: bfloat16 [768], replicated, may hold values from 0.5 to 1.5
- mid_shift: bfloat16 [768], replicated, may hold values from -3 to 3
- up_weight: bfloat16 [768, 3072], P(None, 'mp'), may hold values from -0.21875 to 0.21875
- up_bias: bfloat16 [3072], P('mp'), may hold values from -3 to 3
- down_weight: bfloat16 [3072, 768], P('mp'), may hold values from -0.15625 to 0.15625
- down_bias: bfloat16 [768], replicated, may hold values from -3 to 3
- final_gain: bfloat16 [768], replicated, may hold values from 0.5 to 1.5
- final_shift: bfloat16 [768], replicated, may hold values from -3 to 3
Outputs:
- layer_out: bfloat16 [8192, 768], P('dp')
- input_grad: bfloat16 [8192, 768], P('dp')
- query_weight_grad: float32 [768, 768], P(None, 'mp')
- query_bias_grad: float32 [768], P('mp')
- key_weight_grad: float32 [768, 768], P(None, 'mp')
- value_weight_grad: float32 [768, 768], P(None, 'mp')
- value_bias_grad: float32 [768], P('mp')
- out_weight_grad: float32 [768, 768], P('mp')
- out_bias_grad: float32 [768], replicated
- mid_gain_grad: float32 [768], replicated
- mid_shift_grad: float32 [768], replicated
- up_weight_grad: float32 [768, 3072], P(None, 'mp')
- up_bias_grad: float32 [3072], P('mp')
- down_weight_grad: float32 [3072, 768], P('mp')
- down_bias_grad: float32 [768], replicated
- final_gain_grad: float32 [768], replicated
- final_shift_grad: float32 [768], replicated
Inputs may be any that keep to these rules, and one draw needn't show every extreme that they name: `lengths`: real tokens of each page; key slots at or beyond it are padding. Some page has exactly 512 and some exactly 40.
All inputs are finite; a program needn't handle non-finite values.
Results may differ from a plain program's by a relative error of at most 0.015.
The roundings to bfloat16 on the way count: a program that leaves them out, or rounds other values in their place, can miss the bound.
Values sent between devices are 32-bit elements; how exact they have to be, the bound alone decides.
No kernel may reach another device: no remote copies, remote signals or barrier semaphores. Data moves between devices by JAX's collectives and lax.ppermute only.
A program may use at most 128 MiB of HBM per device.

v0:
```python
import functools

import jax
import jax.numpy as jnp
import numpy as np
from jax import lax
from jax.experimental import pallas as pl
from jax.experimental.pallas import tpu as pltpu
from jax.sharding import PartitionSpec as P

DH = 64
BLOCK = 384
HALF = 192
CUBE = 16
MIB = 1 << 20

norm_eps = 1e-12
score_scale = 0.125
root_half = 0.7071067811865476
inv_root_two_pi = 0.3989422804014327

PLAN = {"D": "Q", "E": "P", "U": "P", "V": "P", "R": "S", "S": "P"}
ORDER = (
    ("D1", "E1", "keep", "ffn", "V1", "mid", "back", "tail", "E2", "D2", "V2", "cut", "S1", "U1", "E3", "V3"),
    ("R1", "E4", "D3", "V4", "E5", "R2", "E6", "D4", "V5", "S2", "R3", "U2", "R4", "D5", "V6", "S3"),
    ("U3", "E7", "R5", "V7", "S4", "R6", "D6", "U4", "S5", "Vj", "fin", "R7", "U5", "S6", "D7", "Ej"),
    ("U6", "S7", "Rj", "U7", "Sj", "Dj", "vec", "Uj"),
)
ROUTES = {
    "P": ((1, 2), (2, 1), (4, 4)),
    "S": ((1, 2), (4, 4), (2, 1)),
    "Q": ((4, 4), (1, 2), (2, 1)),
}
ACROSS = (12, 12)


def coordinate(rank, mask):
    if mask == 1:
        return rank & 1
    if mask == 2:
        return (rank >> 1) & 1
    return ((rank >> 2) ^ (rank >> 3)) & 1


def block_places(name):
    sub = HALF * (name in "EVS")
    places = []
    for block in range(8):
        high, low = block >> 1, block & 1
        if name in "DE":
            row, column = high * BLOCK + sub, low * BLOCK
            places.append((0, row, column, row, column))
        elif name in "UV":
            row, column = low * BLOCK + sub, high * BLOCK
            places.append((0, row, column, row, column))
        elif high < 3:
            row = low * BLOCK + sub
            places.append((high, row, 0, row, high * BLOCK))
        else:
            places.append((3, sub, low * BLOCK, 2 * BLOCK + sub, (3 + low) * BLOCK))
    return places


def device_tables(ranks):
    rows = []
    for rank in range(ranks):
        for core in range(2):
            row = []
            for name, route in PLAN.items():
                first, second, third = [coordinate(rank, pair[core]) for pair in ROUTES[route]]
                mine = 4 * first + 2 * second + third
                places = block_places(name)
                row += [places[spot ^ mine][3] for spot in range(8)]
                row += [places[spot ^ mine][4] for spot in range(8)]
                near = [(block ^ mine) & 3 for block in range(8)]
                far = list(near)
                for block in range(8):
                    edge = 4 if block < 4 else 3
                    if block >> 2 == first:
                        far[block] = near[edge]
                    else:
                        near[block] = (edge ^ mine) & 3
                row += near + far + [first]
            rows.append(row)
    return np.array(rows, np.int32)


TABLE = 33
PIECES = 4


def matmul(left, right):
    return jnp.dot(left, right, preferred_element_type=jnp.float32)


def matmul_flip(left, right):
    return lax.dot_general(
        left, right, (((1,), (1,)), ((), ())), preferred_element_type=jnp.float32
    )


def outer_sum(left, right):
    return lax.dot_general(
        left, right, (((0,), (0,)), ((), ())), preferred_element_type=jnp.float32
    )


def wide(ref):
    return ref[...].astype(jnp.float32)


def across(ref):
    return wide(ref).reshape(1, -1)


def row_mean(value):
    return jnp.mean(value, axis=-1, keepdims=True)


def norm_parts(value):
    center = value - row_mean(value)
    scale = lax.rsqrt(row_mean(center * center) + norm_eps)
    return center * scale, scale


def norm_lower(along, normal, scale):
    return scale * (along - row_mean(along) - normal * row_mean(along * normal))


def column_sum(value):
    return jnp.sum(value, axis=0, keepdims=True)


def cost(flops, bytes_accessed, transcendentals=0):
    return pl.CostEstimate(flops=1, bytes_accessed=1, transcendentals=0)


def call(kernel, ins, outs, estimate, limit, scalars=1, scratch=()):
    specs = [
        pl.BlockSpec(memory_space=pltpu.SMEM if place < scalars else pltpu.VMEM)
        for place in range(len(ins))
    ]
    return pl.pallas_call(
        kernel,
        out_shape=tuple(jax.ShapeDtypeStruct(shape, kind) for shape, kind in outs),
        in_specs=specs,
        out_specs=tuple(pl.BlockSpec(memory_space=pltpu.VMEM) for _ in outs),
        scratch_shapes=list(scratch),
        compiler_params=pltpu.CompilerParams(vmem_limit_bytes=limit * MIB),
        cost_estimate=estimate,
    )(*ins)


class Arrival:
    def __init__(self, source, target, sem):
        self.target = target
        self.copy = pltpu.make_async_copy(source, target, sem)
        self.copy.start()
        self.here = False
        self.shape = target.shape

    def wait(self):
        if not self.here:
            self.copy.wait()
            self.here = True

    def __getitem__(self, place):
        self.wait()
        return self.target[place]


class Departure:
    def __init__(self, source, target, sem):
        self.source = source
        self.copy = pltpu.make_async_copy(source, target, sem)
        self.shape = source.shape

    def __getitem__(self, place):
        return self.source[place]

    def __setitem__(self, place, value):
        self.source[place] = value

    def send(self):
        self.copy.start()


def mixed(kernel, ins, far_ins, outs, far_outs, estimate, limit, scalars=0, scratch=()):
    far_in = [pltpu.with_memory_space_constraint(array, pltpu.HBM) for array in far_ins]
    near_count, far_count, near_outs = len(ins), len(far_ins), len(outs)

    def body(*refs):
        near, refs = refs[:near_count], refs[near_count:]
        sources, refs = refs[:far_count], refs[far_count:]
        results, refs = refs[:near_outs], refs[near_outs:]
        targets, refs = refs[: len(far_outs)], refs[len(far_outs) :]
        held, refs = refs[:far_count], refs[far_count:]
        kept, refs = refs[: len(far_outs)], refs[len(far_outs) :]
        in_sem, out_sem = refs[:2]
        arrivals = [Arrival(sources[k], held[k], in_sem.at[k]) for k in range(far_count)]
        departures = [Departure(kept[k], targets[k], out_sem.at[k]) for k in range(len(far_outs))]
        kernel(*near, *arrivals, *results, *departures, *refs[2:])
        for departure in departures:
            departure.copy.wait()

    far, close = pl.BlockSpec(memory_space=pltpu.HBM), pl.BlockSpec(memory_space=pltpu.VMEM)
    small = pl.BlockSpec(memory_space=pltpu.SMEM)
    return pl.pallas_call(
        body,
        out_shape=tuple(jax.ShapeDtypeStruct(shape, kind) for shape, kind in outs)
        + tuple(pltpu.HBM(shape, kind) for shape, kind in far_outs),
        in_specs=[small] * scalars + [close] * (near_count - scalars) + [far] * far_count,
        out_specs=tuple([close] * near_outs + [far] * len(far_outs)),
        scratch_shapes=[pltpu.VMEM(array.shape, array.dtype) for array in far_ins]
        + [pltpu.VMEM(shape, kind) for shape, kind in far_outs]
        + [pltpu.SemaphoreType.DMA((max(1, far_count),)), pltpu.SemaphoreType.DMA((max(1, len(far_outs)),))]
        + list(scratch),
        compiler_params=pltpu.CompilerParams(vmem_limit_bytes=limit * MIB),
        cost_estimate=estimate,
    )(*ins, *far_in)


def head_of(lanes, head):
    return (lanes // DH) == head


def scores_flip(keys, query, limit):
    scores = matmul_flip(keys, query)
    visible = lax.broadcasted_iota(jnp.int32, scores.shape, 0) < limit
    return jnp.where(visible, scores, -1e30)


def attend_kernel(
    lengths, inputs, query_weight, query_bias, key_weight, value_weight, value_bias, out_weight, out_bias,
    partial_ref, query_ref, keys_ref, values_ref, context_ref, log_ref,
):
    query_ref[...] = (matmul(inputs[...], query_weight[...]) + across(query_bias)).astype(jnp.bfloat16)
    query_ref.send()
    keys_ref[...] = matmul(inputs[...], key_weight[...]).astype(jnp.bfloat16)
    keys_ref.send()
    values_ref[...] = (matmul(inputs[...], value_weight[...]) + across(value_bias)).astype(jnp.bfloat16)
    values_ref.send()
    limit = lengths[0]
    for pair in range(query_ref.shape[1] // (2 * DH)):
        columns = slice(pair * 2 * DH, (pair + 1) * 2 * DH)
        query = query_ref[:, columns] * jnp.bfloat16(score_scale)
        keys = keys_ref[:, columns]
        values = values_ref[:, columns]
        lanes = lax.broadcasted_iota(jnp.int32, query.shape, 1)
        sides = []
        for head in range(2):
            scores = scores_flip(keys, jnp.where(head_of(lanes, head), query, 0), limit)
            top = jnp.max(scores, axis=0, keepdims=True)
            raised = jnp.exp(scores - top)
            total = jnp.sum(raised, axis=0, keepdims=True)
            chances = (raised * (1.0 / total)).astype(jnp.bfloat16)
            log_ref[2 * pair + head : 2 * pair + head + 1, :] = top + jnp.log(total)
            sides.append(outer_sum(values, chances))
        rows = lax.broadcasted_iota(jnp.int32, sides[0].shape, 0)
        context = jnp.where(head_of(rows, 0), sides[0], sides[1])
        context_ref[:, columns] = context.T.astype(jnp.bfloat16)
    context_ref.send()
    log_ref.send()
    partial_ref[...] = matmul(context_ref[...], out_weight[...]) + 0.5 * across(out_bias)


def attend(
    lengths, tokens, query_weight, query_bias, key_weight, value_weight, value_bias, out_weight, out_bias
):
    rows, width = tokens.shape
    columns = query_weight.shape[1]
    partial, query, keys, values, context, log_total = mixed(
        attend_kernel,
        (lengths,),
        (tokens, query_weight, query_bias, key_weight, value_weight, value_bias, out_weight, out_bias),
        (((rows, width), jnp.float32),),
        [((rows, columns), jnp.bfloat16)] * 4 + [((8, rows), jnp.float32)],
        cost(8 * rows * width * columns + 8 * rows * rows * columns, 8 * MIB),
        limit=20,
        scalars=1,
    )
    return query, keys, values, context, log_total, partial


def phi(before):
    return 0.5 * (1.0 + lax.erf(before * root_half))


def ffn_kernel(
    tokens, own, got, up_weight, mid_gain, mid_shift, up_bias, down_weight, down_bias,
    partial_ref, middle_ref, normal_ref, scale_ref, low_ref, flipped_ref, active,
):
    normal, scale = norm_parts(wide(tokens) + (own[...] + got[...]))
    middle = normal * across(mid_gain) + across(mid_shift)
    middle_ref[...] = middle
    middle_ref.send()
    low_ref[...] = middle.astype(jnp.bfloat16)
    low_ref.send()
    normal_ref[...] = normal
    normal_ref.send()
    scale_ref[...] = scale
    scale_ref.send()
    hidden = up_weight.shape[1]
    bias = across(up_bias)
    for start in range(0, hidden, 256):
        columns = slice(start, start + 256)
        before = matmul(low_ref[...], up_weight[:, columns]) + bias[:, columns]
        active[:, columns] = (before * phi(before)).astype(jnp.bfloat16)
    flip_into(flipped_ref, active)
    flipped_ref.send()
    partial_ref[...] = matmul(active[...], down_weight[...]) + 0.5 * across(down_bias)


def ffn(tokens, own, got, mid_gain, mid_shift, up_weight, up_bias, down_weight, down_bias):
    rows, width = tokens.shape
    hidden = up_weight.shape[1]
    full = ((rows, width), jnp.float32)
    return mixed(
        ffn_kernel,
        (tokens, own, got, up_weight),
        (mid_gain, mid_shift, up_bias, down_weight, down_bias),
        (full,),
        (full, full, ((rows, 1), jnp.float32), ((rows, width), jnp.bfloat16), ((hidden, rows), jnp.bfloat16)),
        cost(4 * rows * width * hidden, 16 * MIB, rows * hidden),
        limit=26,
        scratch=[pltpu.VMEM((rows, hidden), jnp.bfloat16)],
    )


def cut(offsets, flipped, right, targets, first, spots):
    for part in range(2):
        base = (first + part) * TABLE
        for place, spot in enumerate(spots):
            row = pl.multiple_of(offsets[base + spot], HALF // 12)
            column = pl.multiple_of(offsets[base + 8 + spot], 128)
            targets[part][place * HALF : (place + 1) * HALF, :] = matmul(
                flipped[pl.ds(row, HALF), :], right[:, pl.ds(column, BLOCK)]
            )


KEPT = (0, 1, 2, 3)
SENT = (4, 5, 6, 7)


def flip_into(flipped, left, start=0):
    for column in range(0, left.shape[1], 128):
        flipped[start + column : start + column + 128, :] = left[:, column : column + 128].T


SUMS = 16
blocks = ((4 * HALF, BLOCK), jnp.float32)
blocks_and_sums = ((4 * HALF + 2 * SUMS, BLOCK), jnp.float32)


def sums(width):
    return ((8, width), jnp.float32)


def last_kernel(
    offsets, middle, own, got, cotangent, final_gain, flipped,
    second_ref, low_ref, final_ref, send0, send1,
):
    final, scale = norm_parts(middle[...] + (own[...] + got[...]))
    final_ref[...] = final
    second = norm_lower(wide(cotangent) * across(final_gain), final, scale)
    low_ref[...] = second.astype(jnp.bfloat16)
    second_ref[...] = second
    flipped.wait()
    cut(offsets, flipped.target, low_ref, (send0, send1), 0, SENT)


def last(offsets, middle, own, got, cotangent, final_gain, flipped):
    rows, width = middle.shape
    full = ((rows, width), jnp.float32)
    return mixed(
        last_kernel,
        (offsets, middle, own, got),
        (cotangent, final_gain, flipped),
        (full, ((rows, width), jnp.bfloat16), full, blocks, blocks),
        (),
        cost(rows * width * flipped.shape[0], 14 * MIB),
        limit=24,
        scalars=1,
    )


def keep_kernel(
    offsets, second, low, final, final_gain, final_shift, cotangent, flipped, out_ref, sums_ref, keep0, keep1
):
    cut(offsets, flipped, low, (keep0, keep1), 0, KEPT)
    upper = wide(cotangent)
    sums_ref[...] = jnp.zeros_like(sums_ref)
    sums_ref[0:1, :] = column_sum(second[...])
    sums_ref[1:2, :] = column_sum(upper * final[...])
    sums_ref[2:3, :] = column_sum(upper)
    out_ref[...] = (final[...] * across(final_gain) + across(final_shift)).astype(jnp.bfloat16)


def keep(offsets, second, low, final, final_gain, final_shift, cotangent, flipped):
    rows, width = low.shape
    return call(
        keep_kernel,
        (offsets, second, low, final, final_gain, final_shift, cotangent, flipped),
        (((rows, width), jnp.bfloat16), sums(width), blocks, blocks),
        cost(rows * width * flipped.shape[0], 14 * MIB),
        limit=26,
    )


def ffn_back_kernel(
    offsets, second_low, down_weight, low, up_weight, up_bias,
    sums_ref, send0, keep0, send1, keep1, *rest,
):
    partial_refs, before_grad, flipped = rest[:PIECES], rest[-2], rest[-1]
    hidden = up_weight.shape[1]
    width = sums_ref.shape[1]
    bias = across(up_bias)
    sums_ref[...] = jnp.zeros_like(sums_ref)
    for start in range(0, hidden, 256):
        columns = slice(start, start + 256)
        before = matmul(low[...], up_weight[:, columns]) + bias[:, columns]
        slope = phi(before) + before * inv_root_two_pi * jnp.exp(-0.5 * before * before)
        grad = (matmul_flip(second_low[...], down_weight[columns, :]) * slope).astype(jnp.bfloat16)
        before_grad[:, columns] = grad
        row, place = start // width, start % width
        sums_ref[row : row + 1, place : place + 256] = column_sum(grad.astype(jnp.float32))
    for place, partial_ref in enumerate(partial_refs):
        rows = slice(place * partial_ref.shape[0], (place + 1) * partial_ref.shape[0])
        partial_ref[...] = matmul_flip(before_grad[rows, :], up_weight[...])
    flip_into(flipped, low)
    cut(offsets, flipped, before_grad, (send0, send1), 2, SENT)
    cut(offsets, flipped, before_grad, (keep0, keep1), 2, KEPT)


def ffn_back(offsets, second_low, down_weight, low, up_weight, up_bias):
    rows, width = low.shape
    hidden = up_weight.shape[1]
    return call(
        ffn_back_kernel,
        (offsets, second_low, down_weight, low, up_weight, up_bias),
        (sums(width), blocks, blocks, blocks, blocks) + (((rows // PIECES, width), jnp.float32),) * PIECES,
        cost(6 * rows * width * hidden, 18 * MIB, 2 * rows * hidden),
        scratch=[pltpu.VMEM((rows, hidden), jnp.bfloat16), pltpu.VMEM((width, rows), jnp.bfloat16)],
        limit=26,
    )


def mid_kernel(second, normal_ref, scale, mid_gain, out_weight, *rest):
    own, got = rest[:PIECES], rest[PIECES : 2 * PIECES]
    first_ref, low_ref, context_grad, sums_ref, upper = rest[2 * PIECES :]
    for place in range(PIECES):
        rows = slice(place * own[place].shape[0], (place + 1) * own[place].shape[0])
        upper[rows, :] = second[rows, :] + (own[place][...] + got[place][...])
    normal = normal_ref[...]
    sums_ref[...] = jnp.zeros_like(sums_ref)
    sums_ref[1:2, :] = column_sum(upper[...] * normal)
    sums_ref[2:3, :] = column_sum(upper[...])
    first = norm_lower(upper[...] * across(mid_gain), normal, scale[...])
    sums_ref[0:1, :] = column_sum(first)
    first_ref[...] = first
    low_ref[...] = first.astype(jnp.bfloat16)
    context_grad[...] = matmul_flip(low_ref[...], out_weight[...]).astype(jnp.bfloat16)


def mid(second, own, got, normal, scale, mid_gain, out_weight):
    rows, width = second.shape
    columns = out_weight.shape[0]
    return call(
        mid_kernel,
        (second, normal, scale, mid_gain, out_weight, *own, *got),
        (
            ((rows, width), jnp.float32),
            ((rows, width), jnp.bfloat16),
            ((rows, columns), jnp.bfloat16),
            sums(width),
        ),
        cost(2 * rows * width * columns, 10 * MIB),
        scalars=0,
        scratch=[pltpu.VMEM((rows, width), jnp.float32)],
        limit=20,
    )


def attend_back_kernel(
    lengths, query_ref, keys_ref, values_ref, log_ref, upstream_ref,
    grads_ref, sums_ref,
):
    limit = lengths[0]
    sums_ref[...] = jnp.zeros_like(sums_ref)
    width = query_ref.shape[1]
    @pl.loop(0, width // (2 * DH))
    def _(pair):
        start = pl.multiple_of(pair * 2 * DH, 2 * DH)
        columns = pl.ds(start, 2 * DH)
        query = query_ref[:, columns] * jnp.bfloat16(score_scale)
        keys = keys_ref[:, columns]
        values = values_ref[:, columns]
        upstream = upstream_ref[:, columns]
        lanes = lax.broadcasted_iota(jnp.int32, query.shape, 1)
        value_grad = jnp.zeros(query.shape, jnp.float32)
        key_grad = jnp.zeros(query.shape, jnp.float32)
        sides = []
        for head in range(2):
            mine = head_of(lanes, head)
            asked = jnp.where(mine, query, 0)
            pulled = jnp.where(mine, upstream, 0)
            scores = scores_flip(keys, asked, limit)
            chances = jnp.exp(scores - log_ref[pl.ds(2 * pair + head, 1), :])
            value_grad = value_grad + matmul(chances.astype(jnp.bfloat16), pulled)
            spread = matmul_flip(values, pulled).astype(jnp.bfloat16).astype(jnp.float32)
            common = jnp.sum(spread * chances, axis=0, keepdims=True)
            score_grad = (chances * (spread - common)).astype(jnp.bfloat16)
            key_grad = key_grad + matmul(score_grad, asked)
            sides.append(outer_sum(keys, score_grad))
        rows = lax.broadcasted_iota(jnp.int32, sides[0].shape, 0)
        query_grad = (jnp.where(head_of(rows, 0), sides[0], sides[1]).T * score_scale).astype(jnp.bfloat16)
        key_low = key_grad.astype(jnp.bfloat16)
        value_low = value_grad.astype(jnp.bfloat16)
        grads_ref[:, columns] = query_grad
        grads_ref[:, pl.ds(width + start, 2 * DH)] = key_low
        grads_ref[:, pl.ds(2 * width + start, 2 * DH)] = value_low
        sums_ref[0:1, columns] = column_sum(query_grad.astype(jnp.float32))
        sums_ref[0:1, pl.ds(width + start, 2 * DH)] = column_sum(
            value_low.astype(jnp.float32)
        )


def attend_back(lengths, query, keys, values, log_total, upstream):
    rows, width = query.shape
    return call(
        attend_back_kernel,
        (lengths, query, keys, values, log_total, upstream),
        (((rows, 3 * width), jnp.bfloat16), sums(2 * width)),
        cost(20 * rows * rows * width, 4 * MIB, rows * rows * width // DH),
        limit=16,
    )


def rest_kernel(
    offsets, tokens, context, grads, first_low, last_sums, up_sums, mid_sums, back_sums,
    send0, keep0, send1, keep1, flipped, right,
):
    flip_into(flipped, tokens)
    flip_into(flipped, context, tokens.shape[1])
    right[:, : grads.shape[1]] = grads[...]
    right[:, grads.shape[1] :] = first_low[...]
    cut(offsets, flipped, right, (send0, send1), 4, SENT)
    cut(offsets, flipped, right, (keep0, keep1), 4, KEPT)
    rows = [last_sums[0:3, :], up_sums[0:2, :], mid_sums[0:3, :], back_sums[0:1, :]]
    send1[4 * HALF :, :] = jnp.zeros((2 * SUMS, BLOCK), jnp.float32)
    for half in range(2):
        place = 4 * HALF + half * SUMS
        for part in rows:
            send1[place : place + part.shape[0], :] = part[:, half * BLOCK : (half + 1) * BLOCK]
            place = place + part.shape[0]


def rest(offsets, tokens, context, grads, first_low, last_sums, up_sums, mid_sums, back_sums):
    rows, width = tokens.shape
    left = width + context.shape[1]
    right = grads.shape[1] + width
    return call(
        rest_kernel,
        (offsets, tokens, context, grads, first_low, last_sums, up_sums, mid_sums, back_sums),
        (blocks, blocks, blocks_and_sums, blocks),
        cost(32 * rows * HALF * BLOCK, 8 * MIB),
        scratch=[pltpu.VMEM((left, rows), jnp.bfloat16), pltpu.VMEM((rows, right), jnp.bfloat16)],
        limit=16,
    )


def input_kernel(grads, query_weight, key_weight, value_weight, partial_ref):
    width = query_weight.shape[1]
    partial_ref[...] = (
        matmul_flip(grads[:, :width], query_weight[...])
        + matmul_flip(grads[:, width : 2 * width], key_weight[...])
        + matmul_flip(grads[:, 2 * width :], value_weight[...])
    )


def input_part(grads, query_weight, key_weight, value_weight):
    rows, width = grads.shape[0], query_weight.shape[0]
    return call(
        input_kernel,
        (grads, query_weight, key_weight, value_weight),
        (((rows, width), jnp.float32),),
        cost(2 * rows * width * grads.shape[1], 6 * MIB),
        scalars=0,
        limit=10,
    )[0]


def join_kernel(name, table, near, far, *rest):
    places = block_places(name)
    count = len({place[0] for place in places})
    outs, done = rest[-count - 1 : -1], rest[-1]
    for side in range(2):

        @pl.when(table[16] == side)
        def _():
            copies = []
            for block in range(8):
                out, row, column = places[block][:3]
                source = near if block >> 2 == side else far
                copies.append(
                    pltpu.make_async_copy(
                        source.at[pl.ds(pl.multiple_of(table[8 * (source is far) + block] * HALF, 8), HALF)],
                        outs[out].at[pl.ds(row, HALF), pl.ds(column, BLOCK)],
                        done.at[block],
                    )
                )
            for copy in copies:
                copy.start()
            for copy in copies:
                copy.wait()


def join(name, table, near, far, shapes, earlier):
    specs = [
        pl.BlockSpec(memory_space=pltpu.SMEM),
        pl.BlockSpec(memory_space=pltpu.VMEM),
        pl.BlockSpec(memory_space=pltpu.VMEM),
    ] + [pl.BlockSpec(memory_space=pl.ANY) for _ in earlier]
    return pl.pallas_call(
        functools.partial(join_kernel, name),
        out_shape=tuple(jax.ShapeDtypeStruct(shape, jnp.float32) for shape in shapes),
        in_specs=specs,
        out_specs=tuple(pl.BlockSpec(memory_space=pl.ANY) for _ in shapes),
        scratch_shapes=[pltpu.SemaphoreType.DMA((8,))],
        input_output_aliases={3 + place: place for place in range(len(earlier))},
        compiler_params=pltpu.CompilerParams(vmem_limit_bytes=16 * MIB),
        cost_estimate=cost(0, 64 * HALF * BLOCK),
    )(table, near, far, *earlier)


def swap_cores(part):
    return lax.ppermute(part, "mp", [(0, 1), (1, 0)])


def hop(block, masks, ranks):
    pairs = [
        (2 * rank + core, 2 * (rank ^ masks[core]) + core) for rank in range(ranks) for core in (0, 1)
    ]
    return lax.ppermute(block, ("dp", "mp"), pairs)


def tied(value, before):
    return value if before is None else lax.optimization_barrier((value, before))[0]


class Sum:
    def __init__(self, name, send, keep, ranks):
        self.name, self.send, self.keep, self.ranks = name, send, keep, ranks
        self.masks = ROUTES[PLAN[name]] + (ACROSS,)
        self.got = {}
        self.extra = send[4 * HALF :] if send.shape[0] > 4 * HALF else None

    def with_extra(self, value, got, rows):
        if self.extra is None:
            return value
        self.extra = self.extra + got[rows:]
        return jnp.concatenate([value, self.extra])

    def step(self, number, before):
        got, one, two = self.got, HALF, 2 * HALF
        keep = tied(self.own if number > 4 else self.keep if number > 1 else self.send, before)
        if number == 1:
            value = keep
        elif number == 2:
            value = self.with_extra(keep[two:] + got[1][two : 2 * two], got[1], 2 * two)
        elif number == 3:
            value = self.with_extra(keep[one:two] + got[1][one:two] + got[2][one:two], got[2], two)
        elif number == 4:
            value = keep[:one] + got[1][:one] + got[2][:one] + got[3][:one]
            value = self.with_extra(value, got[3], one)
        elif number == 5:
            value = keep + got[4]
            bit = CUBE
            while bit < self.ranks:
                value = value + hop(value, (bit, bit), self.ranks)
                bit = 2 * bit
            if self.extra is not None:
                value, self.extra = value[:one], value[one:]
        elif number == 6:
            value = jnp.concatenate([keep, got[5]])
        else:
            value = jnp.concatenate([keep, got[6]])
        self.own = value
        with jax.named_scope(f"{self.name}{number}"):
            got[number] = hop(value, self.masks[min(number, 8 - number) - 1], self.ranks)
        return value


def body(
    ranks,
    tables,
    tokens,
    lengths,
    cotangent,
    query_weight,
    query_bias,
    key_weight,
    value_weight,
    value_bias,
    out_weight,
    out_bias,
    mid_gain,
    mid_shift,
    up_weight,
    up_bias,
    down_weight,
    down_bias,
    final_gain,
    final_shift,
):
    table = jnp.asarray(tables)[2 * lax.axis_index("dp") + lax.axis_index("mp")]
    width = tokens.shape[1]
    columns = query_weight.shape[1]
    hidden = up_weight.shape[1]

    query, keys, values, context, log_total, partial = attend(
        lengths, tokens, query_weight, query_bias, key_weight, value_weight, value_bias, out_weight, out_bias
    )
    down_partial, middle, mid_normal, mid_scale, mid_low, active_flip = ffn(
        tokens, partial, swap_cores(partial), mid_gain, mid_shift, up_weight, up_bias, down_weight, down_bias
    )
    second_grad, second_low, final_normal, *down_sent = last(
        table, middle, down_partial, swap_cores(down_partial), cotangent, final_gain, active_flip
    )
    parts = {
        "D": Sum("D", down_sent[0], None, ranks),
        "E": Sum("E", down_sent[1], None, ranks),
    }
    point = None
    joined = {}
    for item in sum(ORDER, ()):
        if item == "keep":
            layer_out, last_sums, *down_kept = keep(
                table, second_grad, tied(second_low, point), final_normal, final_gain, final_shift,
                cotangent, active_flip,
            )
            parts["D"].keep, parts["E"].keep = down_kept
            point = down_kept[0]
        elif item == "ffn":
            up_sums, *up_cut = ffn_back(
                table, tied(second_low, point), down_weight, mid_low, up_weight, up_bias
            )
            parts["U"] = Sum("U", up_cut[0], up_cut[1], ranks)
            parts["V"] = Sum("V", up_cut[2], up_cut[3], ranks)
            up_partial = up_cut[4:]
            up_got = [swap_cores(piece) for piece in up_partial]
            point = up_cut[0]
        elif item == "mid":
            first_grad, first_low, context_grad, mid_sums = mid(
                tied(second_grad, point), up_partial, up_got, mid_normal, mid_scale, mid_gain, out_weight
            )
            point = context_grad
        elif item == "back":
            grads, back_sums = attend_back(
                lengths, query, keys, values, log_total, tied(context_grad, point)
            )
            point = grads
        elif item == "cut":
            rest_cut = rest(
                table, tokens, context, tied(grads, point), first_low, last_sums, up_sums, mid_sums, back_sums
            )
            parts["R"] = Sum("R", rest_cut[0], rest_cut[1], ranks)
            parts["S"] = Sum("S", rest_cut[2], rest_cut[3], ranks)
            point = rest_cut[0]
        elif item == "tail":
            partial = input_part(tied(grads, point), query_weight, key_weight, value_weight)
            partial_got = swap_cores(partial)
            point = partial
        elif item == "fin":
            input_grad = (first_grad + (tied(partial, point) + partial_got)).astype(jnp.bfloat16)
            point = input_grad
        elif item == "vec":
            small = tied(parts["S"].extra, point).reshape(2, SUMS, BLOCK)
            small = jnp.concatenate([small[0], small[1]], axis=1)
            down_bias_grad, final_gain_grad, final_shift_grad = small[0], small[1], small[2]
            up_bias_grad = small[3 : 3 + hidden // width].reshape(-1)
            out_bias_grad, mid_gain_grad, mid_shift_grad = small[5], small[6], small[7]
            query_bias_grad, value_bias_grad = small[8, :columns], small[8, columns : 2 * columns]
            point = value_bias_grad
        elif item[1] == "j":
            family = {"E": "D", "V": "U", "S": "R"}.get(item[0], item[0])
            shapes = {
                "D": [(hidden, width)],
                "U": [(width, hidden)],
                "R": [(width, columns)] * 3 + [(columns, width)],
            }[family]
            place = list(PLAN).index(item[0]) * TABLE + 16
            part = parts[item[0]]
            joined[family] = join(
                item[0], table[place : place + 17], tied(part.own, point), part.got[7], shapes,
                joined.get(family, ()),
            )
            point = joined[family][0]
        else:
            point = parts[item[0]].step(int(item[1]), point)
    (down_weight_grad,), (up_weight_grad,) = joined["D"], joined["U"]
    query_weight_grad, key_weight_grad, value_weight_grad, out_weight_grad = joined["R"]
    return (
        layer_out,
        input_grad,
        query_weight_grad,
        query_bias_grad,
        key_weight_grad,
        value_weight_grad,
        value_bias_grad,
        out_weight_grad,
        out_bias_grad,
        mid_gain_grad,
        mid_shift_grad,
        up_weight_grad,
        up_bias_grad,
        down_weight_grad,
        down_bias_grad,
        final_gain_grad,
        final_shift_grad,
    )


def solution(mesh):
    rows, whole, split, vector = P("dp", None), P(), P(None, "mp"), P("mp")
    across = P("mp", None)
    in_specs = (
        rows, P("dp"), rows, split, vector, split, split, vector, across, whole, whole, whole,
        split, vector, across, whole, whole, whole,
    )
    out_specs = (
        rows, rows, split, vector, split, split, vector, across, whole, whole, whole,
        split, vector, across, whole, whole, whole,
    )
    ranks = mesh.shape["dp"]
    return jax.shard_map(
        functools.partial(body, ranks, device_tables(ranks)),
        mesh=mesh, in_specs=in_specs, out_specs=out_specs, check_vma=False,
    )
```

profile of v0, /device:TPU:0, one launch (start us, length us, event | category | flops | bytes accessed | tf_op | source)
XLA Modules:
  0.0 250.6 jit_solution(9985823842797852334)
XLA Ops:
  1.3 7.8 %shard_map.314 = (f32[512,768]{1,0:T(8,128)S(1)}, bf16[512,384]{1,0:T(8,128)(2,1)}, bf16[512,384]{1,0:T(8,128)(2,1)}, bf16[512,384]{1,0:T(8,128)(2,1)}, bf16[512,384]{1,0:T(8,128)(2,1)}, /*index=5*/f32[8,512]{1,0:T(8,128)}) custom-call(s32[1]{0:T(128)S(6)} %copy.60.refs_0_.lengths, bf16[512,768]{1,0:T(8,128)(2,1)} %tokens.1, bf16[768,384]{1,0:T(8,128)(2,1)} %query_weight.1, ...), custom_call_target="tpu_custom_call" | custom-call | flops 1 | bytes 1 | tf_op jit(solution)/shard_map/pallas_call | solution.py:208
  9.7 3.0 %collective-permute-done.refs_2_ = f32[512,768]{1,0:T(8,128)S(1)} collective-permute-done((f32[512,768]{1,0:T(8,128)S(1)}, f32[512,768]{1,0:T(8,128)S(1)}, u32[]{:S(2)}, u32[]{:S(2)}) %collective-permute-start) | collective-permute-done | bytes 1572896 | tf_op jit(solution)/shard_map/ppermute | solution.py:637
  12.7 6.6 %shard_map.315 = (f32[512,768]{1,0:T(8,128)}, f32[512,768]{1,0:T(8,128)}, f32[512,768]{1,0:T(8,128)}, f32[512,1]{1,0:T(8,128)}, bf16[512,768]{1,0:T(8,128)(2,1)}, /*index=5*/bf16[1536,512]{1,0:T(8,128)(2,1)}) custom-call(bf16[512,768]{1,0:T(8,128)(2,1)S(1)} %copy-done.2, f32[512,768]{1,0:T(8,128)S(1)} %get-tuple-element.119.refs_1_, ...), custom_call_target="tpu_custom_call" | custom-call | flops 1 | bytes 1 | tf_op jit(solution)/shard_map/pallas_call | solution.py:208
  20.5 2.7 %collective-permute-done.1.refs_3_ = f32[512,768]{1,0:T(8,128)} collective-permute-done((f32[512,768]{1,0:T(8,128)}, f32[512,768]{1,0:T(8,128)}, u32[]{:S(2)}, u32[]{:S(2)}) %collective-permute-start.1) | collective-permute-done | bytes 1572896 | tf_op jit(solution)/shard_map/ppermute | solution.py:637
  24.6 4.8 %shard_map.316 = (f32[512,768]{1,0:T(8,128)S(1)}, bf16[512,768]{1,0:T(8,128)(2,1)S(1)}, f32[512,768]{1,0:T(8,128)S(1)}, f32[768,384]{1,0:T(8,128)S(1)}, f32[768,384]{1,0:T(8,128)S(1)}) custom-call(s32[198]{0:T(256)S(1)} %bitcast.13, f32[512,768]{1,0:T(8,128)S(1)} %copy-done.11, f32[512,768]{1,0:T(8,128)} %get-tuple-element.121.refs_2_, ...), custom_call_target="tpu_custom_call" | custom-call | flops 1 | bytes 1 | tf_op jit(solution)/shard_map/pallas_call | solution.py:208
  29.4 3.1 %collective-permute-start.6 = (f32[768,384]{1,0:T(8,128)S(1)}, f32[768,384]{1,0:T(8,128)S(1)}, u32[]{:S(2)}, u32[]{:S(2)}) collective-permute-start(f32[768,384]{1,0:T(8,128)S(1)} %get-tuple-element.127), channel_id=1, source_target_pairs={{0,2},{1,5},{2,0},{3,7},{4,6},{5,1},{6,4},{7,3},{8,10},{9,13},{10,... | collective-permute-start | bytes 3538952 | tf_op jit(solution)/shard_map/E1/ppermute | solution.py:644
  34.1 3.0 %shard_map.317 = (bf16[512,768]{1,0:T(8,128)(2,1)}, f32[8,768]{1,0:T(8,128)S(1)}, f32[768,384]{1,0:T(8,128)S(1)}, f32[768,384]{1,0:T(8,128)S(1)}) custom-call(s32[198]{0:T(256)S(1)} %bitcast.14, f32[512,768]{1,0:T(8,128)S(1)} %get-tuple-element.137.second, bf16[512,768]{1,0:T(8,128)(2,1)S(1)} %get-tuple-element.132.low.second_low, ...), custom_call_target="tpu_custom_call" | custom-call | flops 1 | bytes 1 | tf_op jit(solution)/shard_map/pallas_call | solution.py:143
  37.2 8.4 %shard_map.318 = (f32[8,768]{1,0:T(8,128)S(1)}, f32[768,384]{1,0:T(8,128)}, f32[768,384]{1,0:T(8,128)S(1)}, f32[768,384]{1,0:T(8,128)S(1)}, f32[768,384]{1,0:T(8...) custom-call(s32[198]{0:T(256)S(1)} %bitcast.15, ...), custom_call_target="tpu_custom_call" | custom-call | flops 1 | bytes 1 | tf_op jit(solution)/shard_map/pallas_call | solution.py:143
  51.3 5.6 %shard_map.320 = (bf16[512,1152]{1,0:T(8,128)(2,1)S(1)}, f32[8,768]{1,0:T(8,128)S(1)}) custom-call(s32[1]{0:T(128)S(6)} %copy.60.refs_0_.lengths, bf16[512,384]{1,0:T(8,128)(2,1)S(1)} %copy-done.20, bf16[512,384]{1,0:T(8,128)(2,1)S(1)} %copy-done.21, bf16[512,384]{1,0:T(8,128)(2,1)S(1)} %copy-done.22, f32[8,512]{1,0:T(8,128)S(1)} %copy-done.24, ...), custom_call_target="tpu_custom_call" | custom-call | flops 1 | bytes 1 | tf_op jit(solution)/shard_map/pallas_call | solution.py:143
  60.3 3.0 %collective-permute-done.8 = f32[768,384]{1,0:T(8,128)S(1)} collective-permute-done((f32[768,384]{1,0:T(8,128)S(1)}, f32[768,384]{1,0:T(8,128)S(1)}, u32[]{:S(2)}, u32[]{:S(2)}) %collective-permute-start.8) | collective-permute-done | bytes 1179680 | tf_op jit(solution)/shard_map/V1/ppermute | solution.py:644
  65.2 2.8 %shard_map.322 = (f32[768,384]{1,0:T(8,128)S(1)}, f32[768,384]{1,0:T(8,128)S(1)}, f32[800,384]{1,0:T(8,128)S(1)}, f32[768,384]{1,0:T(8,128)S(1)}) custom-call(s32[198]{0:T(256)S(1)} %bitcast.16, bf16[512,768]{1,0:T(8,128)(2,1)S(1)} %copy-done.2, bf16[512,384]{1,0:T(8,128)(2,1)S(1)} %copy-done.19, bf16[512,1152]{1,0:T(8,128)(2,1)S(1)} %get-tuple-element.158.grads, ...), custom_call_target="tpu_custom_call" | custom-call | flops 1 | bytes 1 | tf_op jit(solution)/shard_map/pallas_call | solution.py:143
  68.0 1.9 collective-permute-start.19
  69.9 1.8 collective-permute-done.9
  71.9 12.4 %collective-permute-done.10 = f32[384,384]{1,0:T(8,128)S(1)} collective-permute-done((f32[384,384]{1,0:T(8,128)S(1)}, f32[384,384]{1,0:T(8,128)S(1)}, u32[]{:S(2)}, u32[]{:S(2)}) %collective-permute-start.10) | collective-permute-done | bytes 589856 | tf_op jit(solution)/shard_map/V2/ppermute | solution.py:644
  86.7 4.0 %collective-permute-start.14 = (f32[192,384]{1,0:T(8,128)S(1)}, f32[192,384]{1,0:T(8,128)S(1)}, u32[]{:S(2)}, u32[]{:S(2)}) collective-permute-start(f32[192,384]{1,0:T(8,128)S(1)} %fusion.4), channel_id=1, source_target_pairs={{0,24},{1,25},{2,26},{3,27},{4,28},{5,29},{6,30},{7,31},{8,16},{9,... | collective-permute-start | bytes 884744 | tf_op jit(solution)/shard_map/E4/ppermute | solution.py:644
  90.8 4.5 %collective-permute-done.13 = f32[192,384]{1,0:T(8,128)S(1)} collective-permute-done((f32[192,384]{1,0:T(8,128)S(1)}, f32[192,384]{1,0:T(8,128)S(1)}, u32[]{:S(2)}, u32[]{:S(2)}) %collective-permute-start.13) | collective-permute-done | bytes 294944 | tf_op jit(solution)/shard_map/V3/ppermute | solution.py:644
  95.3 2.9 %collective-permute-start.17 = (f32[192,384]{1,0:T(8,128)S(1)}, f32[192,384]{1,0:T(8,128)S(1)}, u32[]{:S(2)}, u32[]{:S(2)}) collective-permute-start(f32[192,384]{1,0:T(8,128)S(1)} %slice_add_fusion.23), channel_id=1, source_target_pairs={{0,4},{1,3},{2,6},{3,1},{4,0},{5,7},{6,2},{7,5},{8,12},{9,11},{10,... | collective-permute-start | bytes 884744 | tf_op jit(solution)/shard_map/D3/ppermute | solution.py:644
  98.3 2.9 %collective-permute-done.14 = f32[192,384]{1,0:T(8,128)S(1)} collective-permute-done((f32[192,384]{1,0:T(8,128)S(1)}, f32[192,384]{1,0:T(8,128)S(1)}, u32[]{:S(2)}, u32[]{:S(2)}) %collective-permute-start.14) | collective-permute-done | bytes 294944 | tf_op jit(solution)/shard_map/E4/ppermute | solution.py:644
  101.9 5.5 %collective-permute-start.16 = (f32[192,384]{1,0:T(8,128)S(1)}, f32[192,384]{1,0:T(8,128)S(1)}, u32[]{:S(2)}, u32[]{:S(2)}) collective-permute-start(f32[192,384]{1,0:T(8,128)S(1)} %add.164), channel_id=1, source_target_pairs={{0,8},{1,9},{2,10},{3,11},{4,12},{5,13},{6,14},{7,15},{8,0},{9,1},... | collective-permute-start | bytes 884744 | tf_op jit(solution)/shard_map/E5/ppermute | solution.py:644
  107.4 2.8 %collective-permute-done.15 = f32[768,384]{1,0:T(8,128)S(1)} collective-permute-done((f32[768,384]{1,0:T(8,128)S(1)}, f32[768,384]{1,0:T(8,128)S(1)}, u32[]{:S(2)}, u32[]{:S(2)}) %collective-permute-start.15) | collective-permute-done | bytes 1179680 | tf_op jit(solution)/shard_map/R1/ppermute | solution.py:644
  111.7 2.6 %collective-permute-done.16 = f32[192,384]{1,0:T(8,128)S(1)} collective-permute-done((f32[192,384]{1,0:T(8,128)S(1)}, f32[192,384]{1,0:T(8,128)S(1)}, u32[]{:S(2)}, u32[]{:S(2)}) %collective-permute-start.16) | collective-permute-done | bytes 294944 | tf_op jit(solution)/shard_map/E5/ppermute | solution.py:644
  120.4 6.5 %collective-permute-done.20 = f32[384,384]{1,0:T(8,128)} collective-permute-done((f32[384,384]{1,0:T(8,128)}, f32[384,384]{1,0:T(8,128)}, u32[]{:S(2)}, u32[]{:S(2)}) %collective-permute-start.20) | collective-permute-done | bytes 589856 | tf_op jit(solution)/shard_map/R2/ppermute | solution.py:644
  133.5 2.7 %collective-permute-done.22 = f32[192,384]{1,0:T(8,128)S(1)} collective-permute-done((f32[192,384]{1,0:T(8,128)S(1)}, f32[192,384]{1,0:T(8,128)S(1)}, u32[]{:S(2)}, u32[]{:S(2)}) %collective-permute-start.22) | collective-permute-done | bytes 294944 | tf_op jit(solution)/shard_map/R3/ppermute | solution.py:644
  138.9 6.4 %collective-permute-start.28 = (f32[192,384]{1,0:T(8,128)S(1)}, f32[192,384]{1,0:T(8,128)S(1)}, u32[]{:S(2)}, u32[]{:S(2)}) collective-permute-start(f32[192,384]{1,0:T(8,128)S(1)} %fusion.1), channel_id=1, source_target_pairs={{0,24},{1,25},{2,26},{3,27},{4,28},{5,29},{6,30},{7,31},{8,16},{9,... | collective-permute-start | bytes 884744 | tf_op jit(solution)/shard_map/R4/ppermute | solution.py:644
  147.2 1.7 collective-permute-done.26
  152.2 1.7 collective-permute-start.33
  156.7 3.1 %collective-permute-done.30 = f32[224,384]{1,0:T(8,128)S(1)} collective-permute-done((f32[224,384]{1,0:T(8,128)S(1)}, f32[224,384]{1,0:T(8,128)S(1)}, u32[]{:S(2)}, u32[]{:S(2)}) %collective-permute-start.30) | collective-permute-done | bytes 344096 | tf_op jit(solution)/shard_map/S3/ppermute | solution.py:644
  161.7 3.7 %collective-permute-done.31 = f32[192,384]{1,0:T(8,128)S(1)} collective-permute-done((f32[192,384]{1,0:T(8,128)S(1)}, f32[192,384]{1,0:T(8,128)S(1)}, u32[]{:S(2)}, u32[]{:S(2)}) %collective-permute-start.31) | collective-permute-done | bytes 294944 | tf_op jit(solution)/shard_map/R5/ppermute | solution.py:644
  166.6 10.3 %collective-permute-start.34 = (f32[224,384]{1,0:T(8,128)S(1)}, f32[224,384]{1,0:T(8,128)S(1)}, u32[]{:S(2)}, u32[]{:S(2)}) collective-permute-start(f32[224,384]{1,0:T(8,128)S(1)} %pad_maximum_fusion.2), channel_id=1, source_target_pairs={{0,24},{1,25},{2,26},{3,27},{4,28},{5,29},{6,30},{7,31},{8,16},{9,... | collective-permute-start | bytes 1032200 | tf_op jit(solution)/shard_map/S4/ppermute | solution.py:644
  177.0 3.0 %collective-permute-start.37 = (f32[384,384]{1,0:T(8,128)S(1)}, f32[384,384]{1,0:T(8,128)S(1)}, u32[]{:S(2)}, u32[]{:S(2)}) collective-permute-start(f32[384,384]{1,0:T(8,128)S(1)} %constant_dynamic-update-slice_fusion.8), channel_id=1, source_target_pairs={{0,8},{1,9},{2,10},{3,11},{4,12},{5,13},{6,14},{7,15},{8,0},{9,1},... | collective-permute-start | bytes 1769480 | tf_op jit(solution)/shard_map/R6/ppermute | solution.py:644
  181.0 3.8 %collective-permute-done.34 = f32[224,384]{1,0:T(8,128)S(1)} collective-permute-done((f32[224,384]{1,0:T(8,128)S(1)}, f32[224,384]{1,0:T(8,128)S(1)}, u32[]{:S(2)}, u32[]{:S(2)}) %collective-permute-start.34) | collective-permute-done | bytes 344096 | tf_op jit(solution)/shard_map/S4/ppermute | solution.py:644
  184.9 4.3 %collective-permute-start.38 = (f32[192,384]{1,0:T(8,128)S(1)}, f32[192,384]{1,0:T(8,128)S(1)}, u32[]{:S(2)}, u32[]{:S(2)}) collective-permute-start(f32[192,384]{1,0:T(8,128)S(1)} %fusion), channel_id=1, source_target_pairs={{0,24},{1,25},{2,26},{3,27},{4,28},{5,29},{6,30},{7,31},{8,16},{9,... | collective-permute-start | bytes 884744 | tf_op jit(solution)/shard_map/U4/ppermute | solution.py:644
  189.3 2.0 shard_map.323.rest_0_
  194.2 4.2 %collective-permute-done.37 = f32[384,384]{1,0:T(8,128)S(1)} collective-permute-done((f32[384,384]{1,0:T(8,128)S(1)}, f32[384,384]{1,0:T(8,128)S(1)}, u32[]{:S(2)}, u32[]{:S(2)}) %collective-permute-start.37) | collective-permute-done | bytes 589856 | tf_op jit(solution)/shard_map/R6/ppermute | solution.py:644
  199.7 1.8 collective-permute-done.39
  201.5 2.2 collective-permute-start.43
  203.7 1.8 collective-permute-done.40
  205.6 2.0 shard_map.324.rest_0_
  207.7 3.0 %collective-permute-start.45 = (f32[384,384]{1,0:T(8,128)S(1)}, f32[384,384]{1,0:T(8,128)S(1)}, u32[]{:S(2)}, u32[]{:S(2)}) collective-permute-start(f32[384,384]{1,0:T(8,128)S(1)} %constant_dynamic-update-slice_fusion.18), channel_id=1, source_target_pairs={{0,4},{1,3},{2,6},{3,1},{4,0},{5,7},{6,2},{7,5},{8,12},{9,11},{10,... | collective-permute-start | bytes 1769480 | tf_op jit(solution)/shard_map/U6/ppermute | solution.py:644
  210.7 7.2 %collective-permute-done.43 = f32[384,384]{1,0:T(8,128)S(1)} collective-permute-done((f32[384,384]{1,0:T(8,128)S(1)}, f32[384,384]{1,0:T(8,128)S(1)}, u32[]{:S(2)}, u32[]{:S(2)}) %collective-permute-start.43) | collective-permute-done | bytes 589856 | tf_op jit(solution)/shard_map/S6/ppermute | solution.py:644
  220.6 2.6 %collective-permute-done.44.far = f32[768,384]{1,0:T(8,128)S(1)} collective-permute-done((f32[768,384]{1,0:T(8,128)S(1)}, f32[768,384]{1,0:T(8,128)S(1)}, u32[]{:S(2)}, u32[]{:S(2)}) %collective-permute-start.44) | collective-permute-done | bytes 1179680 | tf_op jit(solution)/shard_map/R7/ppermute | solution.py:644
  223.2 2.0 shard_map.325
  225.2 5.3 %collective-permute-done.45 = f32[384,384]{1,0:T(8,128)S(1)} collective-permute-done((f32[384,384]{1,0:T(8,128)S(1)}, f32[384,384]{1,0:T(8,128)S(1)}, u32[]{:S(2)}, u32[]{:S(2)}) %collective-permute-start.45) | collective-permute-done | bytes 589856 | tf_op jit(solution)/shard_map/U6/ppermute | solution.py:644
  231.7 4.1 %collective-permute-done.46.far = f32[768,384]{1,0:T(8,128)S(1)} collective-permute-done((f32[768,384]{1,0:T(8,128)S(1)}, f32[768,384]{1,0:T(8,128)S(1)}, u32[]{:S(2)}, u32[]{:S(2)}) %collective-permute-start.46) | collective-permute-done | bytes 1179680 | tf_op jit(solution)/shard_map/S7/ppermute | solution.py:644
  235.8 2.0 shard_map.326
  237.8 2.0 shard_map.327
  241.7 6.7 %collective-permute-done.48.far = f32[768,384]{1,0:T(8,128)S(1)} collective-permute-done((f32[768,384]{1,0:T(8,128)S(1)}, f32[768,384]{1,0:T(8,128)S(1)}, u32[]{:S(2)}, u32[]{:S(2)}) %collective-permute-start.48) | collective-permute-done | bytes 1179680 | tf_op jit(solution)/shard_map/U7/ppermute | solution.py:644
  248.5 2.0 shard_map.328
  (195 shorter events, 57.8 us)
Async XLA Ops:
  9.2 3.6 %collective-permute-start = (f32[512,768]{1,0:T(8,128)S(1)}, f32[512,768]{1,0:T(8,128)S(1)}, u32[]{:S(2)}, u32[]{:S(2)}) collective-permute-start(f32[512,768]{1,0:T(8,128)S(1)} %get-tuple-element.119.refs_1_), channel_id=1, source_target_pairs={{0,1},{1,0},{2,3},{3,2},{4,5},{5,4},{6,7},{7,6},{8,9},{9,8},{10,11... | collective-permute-start | bytes 4718600 | tf_op jit(solution)/shard_map/ppermute | solution.py:637
  19.3 3.8 %collective-permute-start.1 = (f32[512,768]{1,0:T(8,128)}, f32[512,768]{1,0:T(8,128)}, u32[]{:S(2)}, u32[]{:S(2)}) collective-permute-start(f32[512,768]{1,0:T(8,128)} %get-tuple-element.121.refs_2_), channel_id=1, source_target_pairs={{0,1},{1,0},{2,3},{3,2},{4,5},{5,4},{6,7},{7,6},{8,9},{9,8},{10,11... | collective-permute-start | bytes 4718600 | tf_op jit(solution)/shard_map/ppermute | solution.py:637
  29.4 29.0 %collective-permute-start.6 = (f32[768,384]{1,0:T(8,128)S(1)}, f32[768,384]{1,0:T(8,128)S(1)}, u32[]{:S(2)}, u32[]{:S(2)}) collective-permute-start(f32[768,384]{1,0:T(8,128)S(1)} %get-tuple-element.127), channel_id=1, source_target_pairs={{0,2},{1,5},{2,0},{3,7},{4,6},{5,1},{6,4},{7,3},{8,10},{9,13},{10,... | collective-permute-start | bytes 3538952 | tf_op jit(solution)/shard_map/E1/ppermute | solution.py:644
  32.5 27.8 %collective-permute-start.7 = (f32[768,384]{1,0:T(8,128)S(1)}, f32[768,384]{1,0:T(8,128)S(1)}, u32[]{:S(2)}, u32[]{:S(2)}) collective-permute-start(f32[768,384]{1,0:T(8,128)S(1)} %get-tuple-element.126), channel_id=1, source_target_pairs={{0,8},{1,9},{2,10},{3,11},{4,12},{5,13},{6,14},{7,15},{8,0},{9,1},... | collective-permute-start | bytes 3538952 | tf_op jit(solution)/shard_map/D1/ppermute | solution.py:644
  45.6 1.7 collective-permute-start.2
  45.6 2.3 collective-permute-start.3
  46.1 17.2 %collective-permute-start.8 = (f32[768,384]{1,0:T(8,128)S(1)}, f32[768,384]{1,0:T(8,128)S(1)}, u32[]{:S(2)}, u32[]{:S(2)}) collective-permute-start(f32[768,384]{1,0:T(8,128)S(1)} %get-tuple-element.136), channel_id=1, source_target_pairs={{0,2},{1,5},{2,0},{3,7},{4,6},{5,1},{6,4},{7,3},{8,10},{9,13},{10,... | collective-permute-start | bytes 3538952 | tf_op jit(solution)/shard_map/V1/ppermute | solution.py:644
  47.3 1.7 collective-permute-start.4
  58.4 13.3 %collective-permute-start.9 = (f32[384,384]{1,0:T(8,128)S(1)}, f32[384,384]{1,0:T(8,128)S(1)}, u32[]{:S(2)}, u32[]{:S(2)}) collective-permute-start(f32[384,384]{1,0:T(8,128)S(1)} %slice_add_fusion.5), channel_id=1, source_target_pairs={{0,4},{1,3},{2,6},{3,1},{4,0},{5,7},{6,2},{7,5},{8,12},{9,11},{10,... | collective-permute-start | bytes 1769480 | tf_op jit(solution)/shard_map/E2/ppermute | solution.py:644
  63.4 21.0 %collective-permute-start.10 = (f32[384,384]{1,0:T(8,128)S(1)}, f32[384,384]{1,0:T(8,128)S(1)}, u32[]{:S(2)}, u32[]{:S(2)}) collective-permute-start(f32[384,384]{1,0:T(8,128)S(1)} %slice_add_fusion.3), channel_id=1, source_target_pairs={{0,4},{1,3},{2,6},{3,1},{4,0},{5,7},{6,2},{7,5},{8,12},{9,11},{10,... | collective-permute-start | bytes 1769480 | tf_op jit(solution)/shard_map/V2/ppermute | solution.py:644
  64.9 21.7 %collective-permute-start.12 = (f32[384,384]{1,0:T(8,128)S(1)}, f32[384,384]{1,0:T(8,128)S(1)}, u32[]{:S(2)}, u32[]{:S(2)}) collective-permute-start(f32[384,384]{1,0:T(8,128)S(1)} %slice_add_fusion.4), channel_id=1, source_target_pairs={{0,2},{1,5},{2,0},{3,7},{4,6},{5,1},{6,4},{7,3},{8,10},{9,13},{10,... | collective-permute-start | bytes 1769480 | tf_op jit(solution)/shard_map/D2/ppermute | solution.py:644
  68.0 33.8 %collective-permute-start.19 = (f32[800,384]{1,0:T(8,128)S(1)}, f32[800,384]{1,0:T(8,128)S(1)}, u32[]{:S(2)}, u32[]{:S(2)}) collective-permute-start(f32[800,384]{1,0:T(8,128)S(1)} %get-tuple-element.166), channel_id=1, source_target_pairs={{0,2},{1,5},{2,0},{3,7},{4,6},{5,1},{6,4},{7,3},{8,10},{9,13},{10,... | collective-permute-start | bytes 3686408 | tf_op jit(solution)/shard_map/S1/ppermute | solution.py:644
  71.8 14.7 %collective-permute-start.11 = (f32[192,384]{1,0:T(8,128)S(1)}, f32[192,384]{1,0:T(8,128)S(1)}, u32[]{:S(2)}, u32[]{:S(2)}) collective-permute-start(f32[192,384]{1,0:T(8,128)S(1)} %slice_add_fusion.29), channel_id=1, source_target_pairs={{0,8},{1,9},{2,10},{3,11},{4,12},{5,13},{6,14},{7,15},{8,0},{9,1},... | collective-permute-start | bytes 884744 | tf_op jit(solution)/shard_map/E3/ppermute | solution.py:644
  84.4 25.8 %collective-permute-start.15 = (f32[768,384]{1,0:T(8,128)S(1)}, f32[768,384]{1,0:T(8,128)S(1)}, u32[]{:S(2)}, u32[]{:S(2)}) collective-permute-start(f32[768,384]{1,0:T(8,128)S(1)} %get-tuple-element.170), channel_id=1, source_target_pairs={{0,2},{1,5},{2,0},{3,7},{4,6},{5,1},{6,4},{7,3},{8,10},{9,13},{10,... | collective-permute-start | bytes 3538952 | tf_op jit(solution)/shard_map/R1/ppermute | solution.py:644
  85.2 44.2 %collective-permute-start.21 = (f32[768,384]{1,0:T(8,128)}, f32[768,384]{1,0:T(8,128)}, u32[]{:S(2)}, u32[]{:S(2)}) collective-permute-start(f32[768,384]{1,0:T(8,128)} %get-tuple-element.167), channel_id=1, source_target_pairs={{0,2},{1,5},{2,0},{3,7},{4,6},{5,1},{6,4},{7,3},{8,10},{9,13},{10,... | collective-permute-start | bytes 3538952 | tf_op jit(solution)/shard_map/U1/ppermute | solution.py:644
  86.5 8.8 %collective-permute-start.13 = (f32[192,384]{1,0:T(8,128)S(1)}, f32[192,384]{1,0:T(8,128)S(1)}, u32[]{:S(2)}, u32[]{:S(2)}) collective-permute-start(f32[192,384]{1,0:T(8,128)S(1)} %slice_add_fusion.27), channel_id=1, source_target_pairs={{0,8},{1,9},{2,10},{3,11},{4,12},{5,13},{6,14},{7,15},{8,0},{9,1},... | collective-permute-start | bytes 884744 | tf_op jit(solution)/shard_map/V3/ppermute | solution.py:644
  86.7 14.6 %collective-permute-start.14 = (f32[192,384]{1,0:T(8,128)S(1)}, f32[192,384]{1,0:T(8,128)S(1)}, u32[]{:S(2)}, u32[]{:S(2)}) collective-permute-start(f32[192,384]{1,0:T(8,128)S(1)} %fusion.4), channel_id=1, source_target_pairs={{0,24},{1,25},{2,26},{3,27},{4,28},{5,29},{6,30},{7,31},{8,16},{9,... | collective-permute-start | bytes 884744 | tf_op jit(solution)/shard_map/E4/ppermute | solution.py:644
  95.3 19.0 %collective-permute-start.17 = (f32[192,384]{1,0:T(8,128)S(1)}, f32[192,384]{1,0:T(8,128)S(1)}, u32[]{:S(2)}, u32[]{:S(2)}) collective-permute-start(f32[192,384]{1,0:T(8,128)S(1)} %slice_add_fusion.23), channel_id=1, source_target_pairs={{0,4},{1,3},{2,6},{3,1},{4,0},{5,7},{6,2},{7,5},{8,12},{9,11},{10,... | collective-permute-start | bytes 884744 | tf_op jit(solution)/shard_map/D3/ppermute | solution.py:644
  101.2 13.9 %collective-permute-start.18 = (f32[192,384]{1,0:T(8,128)S(1)}, f32[192,384]{1,0:T(8,128)S(1)}, u32[]{:S(2)}, u32[]{:S(2)}) collective-permute-start(f32[192,384]{1,0:T(8,128)S(1)} %fusion.3), channel_id=1, source_target_pairs={{0,24},{1,25},{2,26},{3,27},{4,28},{5,29},{6,30},{7,31},{8,16},{9,... | collective-permute-start | bytes 884744 | tf_op jit(solution)/shard_map/V4/ppermute | solution.py:644
  101.9 12.4 %collective-permute-start.16 = (f32[192,384]{1,0:T(8,128)S(1)}, f32[192,384]{1,0:T(8,128)S(1)}, u32[]{:S(2)}, u32[]{:S(2)}) collective-permute-start(f32[192,384]{1,0:T(8,128)S(1)} %add.164), channel_id=1, source_target_pairs={{0,8},{1,9},{2,10},{3,11},{4,12},{5,13},{6,14},{7,15},{8,0},{9,1},... | collective-permute-start | bytes 884744 | tf_op jit(solution)/shard_map/E5/ppermute | solution.py:644
  111.2 15.6 %collective-permute-start.20 = (f32[384,384]{1,0:T(8,128)}, f32[384,384]{1,0:T(8,128)}, u32[]{:S(2)}, u32[]{:S(2)}) collective-permute-start(f32[384,384]{1,0:T(8,128)} %slice_add_fusion.2), channel_id=1, source_target_pairs={{0,8},{1,9},{2,10},{3,11},{4,12},{5,13},{6,14},{7,15},{8,0},{9,1},... | collective-permute-start | bytes 1769480 | tf_op jit(solution)/shard_map/R2/ppermute | solution.py:644
  116.8 15.3 %collective-permute-start.25 = (f32[416,384]{1,0:T(8,128)}, f32[416,384]{1,0:T(8,128)}, u32[]{:S(2)}, u32[]{:S(2)}) collective-permute-start(f32[416,384]{1,0:T(8,128)} %pad_maximum_fusion), channel_id=1, source_target_pairs={{0,4},{1,3},{2,6},{3,1},{4,0},{5,7},{6,2},{7,5},{8,12},{9,11},{10,... | collective-permute-start | bytes 1916936 | tf_op jit(solution)/shard_map/S2/ppermute | solution.py:644
  119.1 72.2 %collective-permute-start.36 = (f32[512,768]{1,0:T(8,128)S(1)}, f32[512,768]{1,0:T(8,128)S(1)}, u32[]{:S(2)}, u32[]{:S(2)}) collective-permute-start(f32[512,768]{1,0:T(8,128)S(1)} %shard_map.321), channel_id=1, source_target_pairs={{0,1},{1,0},{2,3},{3,2},{4,5},{5,4},{6,7},{7,6},{8,9},{9,8},{10,11... | collective-permute-start | bytes 4718600 | tf_op jit(solution)/shard_map/ppermute | solution.py:637
  119.2 19.8 %collective-permute-start.23 = (f32[192,384]{1,0:T(8,128)}, f32[192,384]{1,0:T(8,128)S(1)}, u32[]{:S(2)}, u32[]{:S(2)}) collective-permute-start(f32[192,384]{1,0:T(8,128)} %fusion.2), channel_id=1, source_target_pairs={{0,24},{1,25},{2,26},{3,27},{4,28},{5,29},{6,30},{7,31},{8,16},{9,... | collective-permute-start | bytes 884744 | tf_op jit(solution)/shard_map/D4/ppermute | solution.py:644
  126.9 18.6 %collective-permute-start.24 = (f32[192,384]{1,0:T(8,128)}, f32[192,384]{1,0:T(8,128)S(1)}, u32[]{:S(2)}, u32[]{:S(2)}) collective-permute-start(f32[192,384]{1,0:T(8,128)} %add.169), channel_id=1, source_target_pairs={{0,8},{1,9},{2,10},{3,11},{4,12},{5,13},{6,14},{7,15},{8,0},{9,1},... | collective-permute-start | bytes 884744 | tf_op jit(solution)/shard_map/V5/ppermute | solution.py:644
  129.4 6.8 %collective-permute-start.22 = (f32[192,384]{1,0:T(8,128)S(1)}, f32[192,384]{1,0:T(8,128)S(1)}, u32[]{:S(2)}, u32[]{:S(2)}) collective-permute-start(f32[192,384]{1,0:T(8,128)S(1)} %slice_add_fusion.17), channel_id=1, source_target_pairs={{0,4},{1,3},{2,6},{3,1},{4,0},{5,7},{6,2},{7,5},{8,12},{9,11},{10,... | collective-permute-start | bytes 884744 | tf_op jit(solution)/shard_map/R3/ppermute | solution.py:644
  132.1 18.4 %collective-permute-start.27 = (f32[384,384]{1,0:T(8,128)S(1)}, f32[384,384]{1,0:T(8,128)S(1)}, u32[]{:S(2)}, u32[]{:S(2)}) collective-permute-start(f32[384,384]{1,0:T(8,128)S(1)} %constant_dynamic-update-slice_fusion), channel_id=1, source_target_pairs={{0,4},{1,3},{2,6},{3,1},{4,0},{5,7},{6,2},{7,5},{8,12},{9,11},{10,... | collective-permute-start | bytes 1769480 | tf_op jit(solution)/shard_map/E6/ppermute | solution.py:644
  136.2 12.6 %collective-permute-start.26 = (f32[384,384]{1,0:T(8,128)S(1)}, f32[384,384]{1,0:T(8,128)S(1)}, u32[]{:S(2)}, u32[]{:S(2)}) collective-permute-start(f32[384,384]{1,0:T(8,128)S(1)} %slice_add_fusion), channel_id=1, source_target_pairs={{0,4},{1,3},{2,6},{3,1},{4,0},{5,7},{6,2},{7,5},{8,12},{9,11},{10,... | collective-permute-start | bytes 1769480 | tf_op jit(solution)/shard_map/U2/ppermute | solution.py:644
  138.9 13.2 %collective-permute-start.28 = (f32[192,384]{1,0:T(8,128)S(1)}, f32[192,384]{1,0:T(8,128)S(1)}, u32[]{:S(2)}, u32[]{:S(2)}) collective-permute-start(f32[192,384]{1,0:T(8,128)S(1)} %fusion.1), channel_id=1, source_target_pairs={{0,24},{1,25},{2,26},{3,27},{4,28},{5,29},{6,30},{7,31},{8,16},{9,... | collective-permute-start | bytes 884744 | tf_op jit(solution)/shard_map/R4/ppermute | solution.py:644
  145.5 9.9 %collective-permute-start.29 = (f32[384,384]{1,0:T(8,128)S(1)}, f32[384,384]{1,0:T(8,128)S(1)}, u32[]{:S(2)}, u32[]{:S(2)}) collective-permute-start(f32[384,384]{1,0:T(8,128)S(1)} %constant_dynamic-update-slice_fusion.2), channel_id=1, source_target_pairs={{0,4},{1,3},{2,6},{3,1},{4,0},{5,7},{6,2},{7,5},{8,12},{9,11},{10,... | collective-permute-start | bytes 1769480 | tf_op jit(solution)/shard_map/V6/ppermute | solution.py:644
  148.8 11.0 %collective-permute-start.30 = (f32[224,384]{1,0:T(8,128)S(1)}, f32[224,384]{1,0:T(8,128)S(1)}, u32[]{:S(2)}, u32[]{:S(2)}) collective-permute-start(f32[224,384]{1,0:T(8,128)S(1)} %pad_maximum_fusion.1), channel_id=1, source_target_pairs={{0,8},{1,9},{2,10},{3,11},{4,12},{5,13},{6,14},{7,15},{8,0},{9,1},... | collective-permute-start | bytes 1032200 | tf_op jit(solution)/shard_map/S3/ppermute | solution.py:644
  150.6 16.0 %collective-permute-start.32 = (f32[192,384]{1,0:T(8,128)S(1)}, f32[192,384]{1,0:T(8,128)S(1)}, u32[]{:S(2)}, u32[]{:S(2)}) collective-permute-start(f32[192,384]{1,0:T(8,128)S(1)} %add.178), channel_id=1, source_target_pairs={{0,4},{1,3},{2,6},{3,1},{4,0},{5,7},{6,2},{7,5},{8,12},{9,11},{10,... | collective-permute-start | bytes 884744 | tf_op jit(solution)/shard_map/D5/ppermute | solution.py:644
  152.2 24.8 %collective-permute-start.33 = (f32[192,384]{1,0:T(8,128)S(1)}, f32[192,384]{1,0:T(8,128)S(1)}, u32[]{:S(2)}, u32[]{:S(2)}) collective-permute-start(f32[192,384]{1,0:T(8,128)S(1)} %slice_add_fusion.11), channel_id=1, source_target_pairs={{0,8},{1,9},{2,10},{3,11},{4,12},{5,13},{6,14},{7,15},{8,0},{9,1},... | collective-permute-start | bytes 884744 | tf_op jit(solution)/shard_map/U3/ppermute | solution.py:644
  155.4 10.1 %collective-permute-start.31 = (f32[192,384]{1,0:T(8,128)S(1)}, f32[192,384]{1,0:T(8,128)S(1)}, u32[]{:S(2)}, u32[]{:S(2)}) collective-permute-start(f32[192,384]{1,0:T(8,128)S(1)} %add.184), channel_id=1, source_target_pairs={{0,4},{1,3},{2,6},{3,1},{4,0},{5,7},{6,2},{7,5},{8,12},{9,11},{10,... | collective-permute-start | bytes 884744 | tf_op jit(solution)/shard_map/R5/ppermute | solution.py:644
  159.8 29.4 %collective-permute-start.35 = (f32[768,384]{1,0:T(8,128)S(1)}, f32[768,384]{1,0:T(8,128)S(1)}, u32[]{:S(2)}, u32[]{:S(2)}) collective-permute-start(f32[768,384]{1,0:T(8,128)S(1)} %constant_dynamic-update-slice_fusion.6.near), channel_id=1, source_target_pairs={{0,2},{1,5},{2,0},{3,7},{4,6},{5,1},{6,4},{7,3},{8,10},{9,13},{10,... | collective-permute-start | bytes 3538952 | tf_op jit(solution)/shard_map/V7/ppermute | solution.py:644
  165.5 40.1 %collective-permute-start.41 = (f32[768,384]{1,0:T(8,128)S(1)}, f32[768,384]{1,0:T(8,128)S(1)}, u32[]{:S(2)}, u32[]{:S(2)}) collective-permute-start(f32[768,384]{1,0:T(8,128)S(1)} %constant_dynamic-update-slice_fusion.4.near), channel_id=1, source_target_pairs={{0,2},{1,5},{2,0},{3,7},{4,6},{5,1},{6,4},{7,3},{8,10},{9,13},{10,... | collective-permute-start | bytes 3538952 | tf_op jit(solution)/shard_map/E7/ppermute | solution.py:644
  166.6 18.3 %collective-permute-start.34 = (f32[224,384]{1,0:T(8,128)S(1)}, f32[224,384]{1,0:T(8,128)S(1)}, u32[]{:S(2)}, u32[]{:S(2)}) collective-permute-start(f32[224,384]{1,0:T(8,128)S(1)} %pad_maximum_fusion.2), channel_id=1, source_target_pairs={{0,24},{1,25},{2,26},{3,27},{4,28},{5,29},{6,30},{7,31},{8,16},{9,... | collective-permute-start | bytes 1032200 | tf_op jit(solution)/shard_map/S4/ppermute | solution.py:644
  177.0 21.4 %collective-permute-start.37 = (f32[384,384]{1,0:T(8,128)S(1)}, f32[384,384]{1,0:T(8,128)S(1)}, u32[]{:S(2)}, u32[]{:S(2)}) collective-permute-start(f32[384,384]{1,0:T(8,128)S(1)} %constant_dynamic-update-slice_fusion.8), channel_id=1, source_target_pairs={{0,8},{1,9},{2,10},{3,11},{4,12},{5,13},{6,14},{7,15},{8,0},{9,1},... | collective-permute-start | bytes 1769480 | tf_op jit(solution)/shard_map/R6/ppermute | solution.py:644
  184.9 13.5 %collective-permute-start.38 = (f32[192,384]{1,0:T(8,128)S(1)}, f32[192,384]{1,0:T(8,128)S(1)}, u32[]{:S(2)}, u32[]{:S(2)}) collective-permute-start(f32[192,384]{1,0:T(8,128)S(1)} %fusion), channel_id=1, source_target_pairs={{0,24},{1,25},{2,26},{3,27},{4,28},{5,29},{6,30},{7,31},{8,16},{9,... | collective-permute-start | bytes 884744 | tf_op jit(solution)/shard_map/U4/ppermute | solution.py:644
  189.2 16.3 %collective-permute-start.40 = (f32[384,384]{1,0:T(8,128)S(1)}, f32[384,384]{1,0:T(8,128)S(1)}, u32[]{:S(2)}, u32[]{:S(2)}) collective-permute-start(f32[384,384]{1,0:T(8,128)S(1)} %constant_dynamic-update-slice_fusion.10), channel_id=1, source_target_pairs={{0,2},{1,5},{2,0},{3,7},{4,6},{5,1},{6,4},{7,3},{8,10},{9,13},{10,... | collective-permute-start | bytes 1769480 | tf_op jit(solution)/shard_map/D6/ppermute | solution.py:644
  191.3 10.2 %collective-permute-start.39 = (f32[192,384]{1,0:T(8,128)S(1)}, f32[192,384]{1,0:T(8,128)S(1)}, u32[]{:S(2)}, u32[]{:S(2)}) collective-permute-start(f32[192,384]{1,0:T(8,128)S(1)} %slice.352), channel_id=1, source_target_pairs={{0,8},{1,9},{2,10},{3,11},{4,12},{5,13},{6,14},{7,15},{8,0},{9,1},... | collective-permute-start | bytes 884744 | tf_op jit(solution)/shard_map/S5/ppermute | solution.py:644
  198.5 9.2 %collective-permute-start.42 = (f32[192,384]{1,0:T(8,128)S(1)}, f32[192,384]{1,0:T(8,128)S(1)}, u32[]{:S(2)}, u32[]{:S(2)}) collective-permute-start(f32[192,384]{1,0:T(8,128)S(1)} %add.195), channel_id=1, source_target_pairs={{0,8},{1,9},{2,10},{3,11},{4,12},{5,13},{6,14},{7,15},{8,0},{9,1},... | collective-permute-start | bytes 884744 | tf_op jit(solution)/shard_map/U5/ppermute | solution.py:644
  198.5 24.6 %collective-permute-start.44 = (f32[768,384]{1,0:T(8,128)S(1)}, f32[768,384]{1,0:T(8,128)S(1)}, u32[]{:S(2)}, u32[]{:S(2)}) collective-permute-start(f32[768,384]{1,0:T(8,128)S(1)} %constant_dynamic-update-slice_fusion.12.near), channel_id=1, source_target_pairs={{0,2},{1,5},{2,0},{3,7},{4,6},{5,1},{6,4},{7,3},{8,10},{9,13},{10,... | collective-permute-start | bytes 3538952 | tf_op jit(solution)/shard_map/R7/ppermute | solution.py:644
  201.5 16.4 %collective-permute-start.43 = (f32[384,384]{1,0:T(8,128)S(1)}, f32[384,384]{1,0:T(8,128)S(1)}, u32[]{:S(2)}, u32[]{:S(2)}) collective-permute-start(f32[384,384]{1,0:T(8,128)S(1)} %constant_dynamic-update-slice_fusion.14), channel_id=1, source_target_pairs={{0,4},{1,3},{2,6},{3,1},{4,0},{5,7},{6,2},{7,5},{8,12},{9,11},{10,... | collective-permute-start | bytes 1769480 | tf_op jit(solution)/shard_map/S6/ppermute | solution.py:644
  207.7 22.9 %collective-permute-start.45 = (f32[384,384]{1,0:T(8,128)S(1)}, f32[384,384]{1,0:T(8,128)S(1)}, u32[]{:S(2)}, u32[]{:S(2)}) collective-permute-start(f32[384,384]{1,0:T(8,128)S(1)} %constant_dynamic-update-slice_fusion.18), channel_id=1, source_target_pairs={{0,4},{1,3},{2,6},{3,1},{4,0},{5,7},{6,2},{7,5},{8,12},{9,11},{10,... | collective-permute-start | bytes 1769480 | tf_op jit(solution)/shard_map/U6/ppermute | solution.py:644
  218.0 17.8 %collective-permute-start.46 = (f32[768,384]{1,0:T(8,128)S(1)}, f32[768,384]{1,0:T(8,128)S(1)}, u32[]{:S(2)}, u32[]{:S(2)}) collective-permute-start(f32[768,384]{1,0:T(8,128)S(1)} %constant_dynamic-update-slice_fusion.20.near), channel_id=1, source_target_pairs={{0,2},{1,5},{2,0},{3,7},{4,6},{5,1},{6,4},{7,3},{8,10},{9,13},{10,... | collective-permute-start | bytes 3538952 | tf_op jit(solution)/shard_map/S7/ppermute | solution.py:644
  219.1 18.8 %collective-permute-start.47 = (f32[768,384]{1,0:T(8,128)S(1)}, f32[768,384]{1,0:T(8,128)S(1)}, u32[]{:S(2)}, u32[]{:S(2)}) collective-permute-start(f32[768,384]{1,0:T(8,128)S(1)} %constant_dynamic-update-slice_fusion.16.near), channel_id=1, source_target_pairs={{0,8},{1,9},{2,10},{3,11},{4,12},{5,13},{6,14},{7,15},{8,0},{9,1},... | collective-permute-start | bytes 3538952 | tf_op jit(solution)/shard_map/D7/ppermute | solution.py:644
  230.6 17.8 %collective-permute-start.48 = (f32[768,384]{1,0:T(8,128)S(1)}, f32[768,384]{1,0:T(8,128)S(1)}, u32[]{:S(2)}, u32[]{:S(2)}) collective-permute-start(f32[768,384]{1,0:T(8,128)S(1)} %constant_dynamic-update-slice_fusion.22.near), channel_id=1, source_target_pairs={{0,2},{1,5},{2,0},{3,7},{4,6},{5,1},{6,4},{7,3},{8,10},{9,13},{10,... | collective-permute-start | bytes 3538952 | tf_op jit(solution)/shard_map/U7/ppermute | solution.py:644
  (34 other events, 326.4 us)
where the time goes:
time: 252 us; the launch traced here: 251 us
  waiting for transfers between devices  95.4 us (38%)
  starting transfers between devices  79 us (31%)
  Pallas kernels  54 us (21%)
  other arithmetic  14.7 us (6%)
  local copies, waits for them, and re-layouts  5.16 us (2%)
    ppermute x42, waiting for transfers between devices, hop(): return lax.ppermute(block, ('dp', 'mp'), pairs)  87.1 us
    ppermute x42, starting transfers between devices, hop(): return lax.ppermute(block, ('dp', 'mp'), pairs)  77.2 us
    pallas_call x6, Pallas kernels, call(): pl.pallas_call(kernel, out_shape=tuple((jax.ShapeDtypeStruct(shape, kind)...  22.7 us
    pallas_call x3, Pallas kernels, mixed(): pl.pallas_call(body, out_shape=tuple((jax.ShapeDtypeStruct(shape, kind) f...  19.2 us
    pallas_call x6, Pallas kernels, join(): pl.pallas_call(functools.partial(join_kernel, name), out_shape=tuple((jax...  12.1 us
    ppermute x7, waiting for transfers between devices, swap_cores(): return lax.ppermute(part, 'mp', [(0, 1), (1, 0)])  8.34 us
  transfers between devices with their start and end apart: 49, of which 29 were waited for; matrix products, arithmetic and copies ran while one was open for 7% of the time, Pallas kernels for 13%

commit v1 on v0

--- a/solution.py
+++ b/solution.py
@@ -10,7 +10,7 @@
 
 DH = 64
 BLOCK = 384
-HALF = 192
+ROWS = {"D": (0, 192), "E": (192, 192), "U": (0, 176), "V": (176, 208), "R": (0, 176), "S": (176, 208)}
 CUBE = 16
 MIB = 1 << 20
 
@@ -23,7 +23,7 @@
 ORDER = (
     ("D1", "E1", "keep", "ffn", "V1", "mid", "back", "tail", "E2", "D2", "V2", "cut", "S1", "U1", "E3", "V3"),
     ("R1", "E4", "D3", "V4", "E5", "R2", "E6", "D4", "V5", "S2", "R3", "U2", "R4", "D5", "V6", "S3"),
-    ("U3", "E7", "R5", "V7", "S4", "R6", "D6", "U4", "S5", "Vj", "fin", "R7", "U5", "S6", "D7", "Ej"),
+    ("U3", "E7", "R5", "V7", "S4", "R6", "U4", "D6", "S5", "Vj", "fin", "R7", "U5", "S6", "D7", "Ej"),
     ("U6", "S7", "Rj", "U7", "Sj", "Dj", "vec", "Uj"),
 )
 ROUTES = {
@@ -43,7 +43,7 @@
 
 
 def block_places(name):
-    sub = HALF * (name in "EVS")
+    sub = ROWS[name][0]
     places = []
     for block in range(8):
         high, low = block >> 1, block & 1
@@ -330,11 +330,12 @@
 def cut(offsets, flipped, right, targets, first, spots):
     for part in range(2):
         base = (first + part) * TABLE
+        rows = ROWS["DEUVRS"[first + part]][1]
         for place, spot in enumerate(spots):
-            row = pl.multiple_of(offsets[base + spot], HALF // 12)
+            row = pl.multiple_of(offsets[base + spot], 16)
             column = pl.multiple_of(offsets[base + 8 + spot], 128)
-            targets[part][place * HALF : (place + 1) * HALF, :] = matmul(
-                flipped[pl.ds(row, HALF), :], right[:, pl.ds(column, BLOCK)]
+            targets[part][place * rows : (place + 1) * rows, :] = matmul(
+                flipped[pl.ds(row, rows), :], right[:, pl.ds(column, BLOCK)]
             )
 
 
@@ -348,8 +349,10 @@
 
 
 SUMS = 16
-blocks = ((4 * HALF, BLOCK), jnp.float32)
-blocks_and_sums = ((4 * HALF + 2 * SUMS, BLOCK), jnp.float32)
+
+
+def blocks(name, more=0):
+    return ((4 * ROWS[name][1] + more, BLOCK), jnp.float32)
 
 
 def sums(width):
@@ -376,7 +379,7 @@
         last_kernel,
         (offsets, middle, own, got),
         (cotangent, final_gain, flipped),
-        (full, ((rows, width), jnp.bfloat16), full, blocks, blocks),
+        (full, ((rows, width), jnp.bfloat16), full, blocks("D"), blocks("E")),
         (),
         cost(rows * width * flipped.shape[0], 14 * MIB),
         limit=24,
@@ -401,7 +404,7 @@
     return call(
         keep_kernel,
         (offsets, second, low, final, final_gain, final_shift, cotangent, flipped),
-        (((rows, width), jnp.bfloat16), sums(width), blocks, blocks),
+        (((rows, width), jnp.bfloat16), sums(width), blocks("D"), blocks("E")),
         cost(rows * width * flipped.shape[0], 14 * MIB),
         limit=26,
     )
@@ -438,7 +441,7 @@
     return call(
         ffn_back_kernel,
         (offsets, second_low, down_weight, low, up_weight, up_bias),
-        (sums(width), blocks, blocks, blocks, blocks) + (((rows // PIECES, width), jnp.float32),) * PIECES,
+        (sums(width), blocks("U"), blocks("U"), blocks("V"), blocks("V")) + (((rows // PIECES, width), jnp.float32),) * PIECES,
         cost(6 * rows * width * hidden, 18 * MIB, 2 * rows * hidden),
         scratch=[pltpu.VMEM((rows, hidden), jnp.bfloat16), pltpu.VMEM((width, rows), jnp.bfloat16)],
         limit=26,
@@ -547,9 +550,10 @@
     cut(offsets, flipped, right, (send0, send1), 4, SENT)
     cut(offsets, flipped, right, (keep0, keep1), 4, KEPT)
     rows = [last_sums[0:3, :], up_sums[0:2, :], mid_sums[0:3, :], back_sums[0:1, :]]
-    send1[4 * HALF :, :] = jnp.zeros((2 * SUMS, BLOCK), jnp.float32)
+    end = send1.shape[0] - 2 * SUMS
+    send1[end:, :] = jnp.zeros((2 * SUMS, BLOCK), jnp.float32)
     for half in range(2):
-        place = 4 * HALF + half * SUMS
+        place = end + half * SUMS
         for part in rows:
             send1[place : place + part.shape[0], :] = part[:, half * BLOCK : (half + 1) * BLOCK]
             place = place + part.shape[0]
@@ -562,8 +566,8 @@
     return call(
         rest_kernel,
         (offsets, tokens, context, grads, first_low, last_sums, up_sums, mid_sums, back_sums),
-        (blocks, blocks, blocks_and_sums, blocks),
-        cost(32 * rows * HALF * BLOCK, 8 * MIB),
+        (blocks("R"), blocks("R"), blocks("S", 2 * SUMS), blocks("S")),
+        cost(16 * rows * BLOCK * BLOCK, 8 * MIB),
         scratch=[pltpu.VMEM((left, rows), jnp.bfloat16), pltpu.VMEM((rows, right), jnp.bfloat16)],
         limit=16,
     )
@@ -592,6 +596,7 @@
 
 def join_kernel(name, table, near, far, *rest):
     places = block_places(name)
+    rows = ROWS[name][1]
     count = len({place[0] for place in places})
     outs, done = rest[-count - 1 : -1], rest[-1]
     for side in range(2):
@@ -604,8 +609,8 @@
                 source = near if block >> 2 == side else far
                 copies.append(
                     pltpu.make_async_copy(
-                        source.at[pl.ds(pl.multiple_of(table[8 * (source is far) + block] * HALF, 8), HALF)],
-                        outs[out].at[pl.ds(row, HALF), pl.ds(column, BLOCK)],
+                        source.at[pl.ds(pl.multiple_of(table[8 * (source is far) + block] * rows, 8), rows)],
+                        outs[out].at[pl.ds(row, rows), pl.ds(column, BLOCK)],
                         done.at[block],
                     )
                 )
@@ -629,7 +634,7 @@
         scratch_shapes=[pltpu.SemaphoreType.DMA((8,))],
         input_output_aliases={3 + place: place for place in range(len(earlier))},
         compiler_params=pltpu.CompilerParams(vmem_limit_bytes=16 * MIB),
-        cost_estimate=cost(0, 64 * HALF * BLOCK),
+        cost_estimate=cost(0, 8 * near.size),
     )(table, near, far, *earlier)
 
 
@@ -653,7 +658,8 @@
         self.name, self.send, self.keep, self.ranks = name, send, keep, ranks
         self.masks = ROUTES[PLAN[name]] + (ACROSS,)
         self.got = {}
-        self.extra = send[4 * HALF :] if send.shape[0] > 4 * HALF else None
+        self.rows = ROWS[name][1]
+        self.extra = send[4 * self.rows :] if send.shape[0] > 4 * self.rows else None
 
     def with_extra(self, value, got, rows):
         if self.extra is None:
@@ -662,7 +668,7 @@
         return jnp.concatenate([value, self.extra])
 
     def step(self, number, before):
-        got, one, two = self.got, HALF, 2 * HALF
+        got, one, two = self.got, self.rows, 2 * self.rows
         keep = tied(self.own if number > 4 else self.keep if number > 1 else self.send, before)
         if number == 1:
             value = keep

time: 252 us -> 250 us (level)
  waiting for transfers between devices: 95.4 us -> 101 us
  starting transfers between devices: 79 us -> 73.6 us
    ppermute x42, starting transfers between devices: 77.2 us -> 71.8 us  [hop(): return lax.ppermute(block, ('dp', 'mp'), pairs)]
    ppermute x42, waiting for transfers between devices: 87.1 us -> 92.2 us  [hop(): return lax.ppermute(block, ('dp', 'mp'), pairs)]
  transfers between devices with their start and end apart: 49 -> 49, of which waited for: 29 -> 28; matrix products, arithmetic and copies ran while one was open for 7% -> 7% of each run, Pallas kernels for 13% -> 13%
where the time goes in v1:
time: 250 us; the launch traced here: 249 us
  waiting for transfers between devices  101 us (40%)
  starting transfers between devices  73.6 us (29%)
  Pallas kernels  53.7 us (21%)
  other arithmetic  14 us (6%)
  local copies, waits for them, and re-layouts  5.16 us (2%)
    ppermute x42, waiting for transfers between devices, hop(): return lax.ppermute(block, ('dp', 'mp'), pairs)  92.2 us
    ppermute x42, starting transfers between devices, hop(): return lax.ppermute(block, ('dp', 'mp'), pairs)  71.8 us
    pallas_call x6, Pallas kernels, call(): pl.pallas_call(kernel, out_shape=tuple((jax.ShapeDtypeStruct(shape, kind)...  22.4 us
    pallas_call x3, Pallas kernels, mixed(): pl.pallas_call(body, out_shape=tuple((jax.ShapeDtypeStruct(shape, kind) f...  19.2 us
    pallas_call x6, Pallas kernels, join(): pl.pallas_call(functools.partial(join_kernel, name), out_shape=tuple((jax...  12 us
    ppermute x7, waiting for transfers between devices, swap_cores(): return lax.ppermute(part, 'mp', [(0, 1), (1, 0)])  8.35 us
  transfers between devices with their start and end apart: 49, of which 28 were waited for; matrix products, arithmetic and copies ran while one was open for 7% of the time, Pallas kernels for 13%

profile of v1, /device:TPU:0, one launch (start us, length us, event | category | flops | bytes accessed | tf_op | source)
XLA Modules:
  0.0 249.3 jit_solution(11107419777830229724)
XLA Ops:
  1.3 7.8 %shard_map.314 = (f32[512,768]{1,0:T(8,128)S(1)}, bf16[512,384]{1,0:T(8,128)(2,1)}, bf16[512,384]{1,0:T(8,128)(2,1)}, bf16[512,384]{1,0:T(8,128)(2,1)}, bf16[512,384]{1,0:T(8,128)(2,1)}, /*index=5*/f32[8,512]{1,0:T(8,128)}) custom-call(s32[1]{0:T(128)S(6)} %copy.60.refs_0_.lengths, bf16[512,768]{1,0:T(8,128)(2,1)} %tokens.1, bf16[768,384]{1,0:T(8,128)(2,1)} %query_weight.1, ...), custom_call_target="tpu_custom_call" | custom-call | flops 1 | bytes 1 | tf_op jit(solution)/shard_map/pallas_call | solution.py:208
  9.7 3.0 %collective-permute-done.refs_2_ = f32[512,768]{1,0:T(8,128)S(1)} collective-permute-done((f32[512,768]{1,0:T(8,128)S(1)}, f32[512,768]{1,0:T(8,128)S(1)}, u32[]{:S(2)}, u32[]{:S(2)}) %collective-permute-start) | collective-permute-done | bytes 1572896 | tf_op jit(solution)/shard_map/ppermute | solution.py:642
  12.7 6.6 %shard_map.315 = (f32[512,768]{1,0:T(8,128)}, f32[512,768]{1,0:T(8,128)}, f32[512,768]{1,0:T(8,128)}, f32[512,1]{1,0:T(8,128)}, bf16[512,768]{1,0:T(8,128)(2,1)}, /*index=5*/bf16[1536,512]{1,0:T(8,128)(2,1)}) custom-call(bf16[512,768]{1,0:T(8,128)(2,1)S(1)} %copy-done.2, f32[512,768]{1,0:T(8,128)S(1)} %get-tuple-element.119.refs_1_, ...), custom_call_target="tpu_custom_call" | custom-call | flops 1 | bytes 1 | tf_op jit(solution)/shard_map/pallas_call | solution.py:208
  20.5 2.7 %collective-permute-done.1.refs_3_ = f32[512,768]{1,0:T(8,128)} collective-permute-done((f32[512,768]{1,0:T(8,128)}, f32[512,768]{1,0:T(8,128)}, u32[]{:S(2)}, u32[]{:S(2)}) %collective-permute-start.1) | collective-permute-done | bytes 1572896 | tf_op jit(solution)/shard_map/ppermute | solution.py:642
  24.6 4.8 %shard_map.316 = (f32[512,768]{1,0:T(8,128)S(1)}, bf16[512,768]{1,0:T(8,128)(2,1)S(1)}, f32[512,768]{1,0:T(8,128)S(1)}, f32[768,384]{1,0:T(8,128)S(1)}, f32[768,384]{1,0:T(8,128)S(1)}) custom-call(s32[198]{0:T(256)S(1)} %bitcast.13, f32[512,768]{1,0:T(8,128)S(1)} %copy-done.11, f32[512,768]{1,0:T(8,128)} %get-tuple-element.121.refs_2_, ...), custom_call_target="tpu_custom_call" | custom-call | flops 1 | bytes 1 | tf_op jit(solution)/shard_map/pallas_call | solution.py:208
  29.4 3.1 %collective-permute-start.6 = (f32[768,384]{1,0:T(8,128)S(1)}, f32[768,384]{1,0:T(8,128)S(1)}, u32[]{:S(2)}, u32[]{:S(2)}) collective-permute-start(f32[768,384]{1,0:T(8,128)S(1)} %get-tuple-element.127), channel_id=1, source_target_pairs={{0,2},{1,5},{2,0},{3,7},{4,6},{5,1},{6,4},{7,3},{8,10},{9,13},{10,... | collective-permute-start | bytes 3538952 | tf_op jit(solution)/shard_map/E1/ppermute | solution.py:649
  34.1 3.0 %shard_map.317 = (bf16[512,768]{1,0:T(8,128)(2,1)}, f32[8,768]{1,0:T(8,128)S(1)}, f32[768,384]{1,0:T(8,128)S(1)}, f32[768,384]{1,0:T(8,128)S(1)}) custom-call(s32[198]{0:T(256)S(1)} %bitcast.14, f32[512,768]{1,0:T(8,128)S(1)} %get-tuple-element.137.second, bf16[512,768]{1,0:T(8,128)(2,1)S(1)} %get-tuple-element.132.low.second_low, ...), custom_call_target="tpu_custom_call" | custom-call | flops 1 | bytes 1 | tf_op jit(solution)/shard_map/pallas_call | solution.py:143
  37.2 8.1 %shard_map.318 = (f32[8,768]{1,0:T(8,128)S(1)}, f32[704,384]{1,0:T(8,128)}, f32[704,384]{1,0:T(8,128)S(1)}, f32[832,384]{1,0:T(8,128)S(1)}, f32[832,384]{1,0:T(8...) custom-call(s32[198]{0:T(256)S(1)} %bitcast.15, ...), custom_call_target="tpu_custom_call" | custom-call | flops 1 | bytes 1 | tf_op jit(solution)/shard_map/pallas_call | solution.py:143
  51.0 5.6 %shard_map.320 = (bf16[512,1152]{1,0:T(8,128)(2,1)S(1)}, f32[8,768]{1,0:T(8,128)S(1)}) custom-call(s32[1]{0:T(128)S(6)} %copy.60.refs_0_.lengths, bf16[512,384]{1,0:T(8,128)(2,1)S(1)} %copy-done.20, bf16[512,384]{1,0:T(8,128)(2,1)S(1)} %copy-done.21, bf16[512,384]{1,0:T(8,128)(2,1)S(1)} %copy-done.22, f32[8,512]{1,0:T(8,128)S(1)} %copy-done.24, ...), custom_call_target="tpu_custom_call" | custom-call | flops 1 | bytes 1 | tf_op jit(solution)/shard_map/pallas_call | solution.py:143
  60.3 4.8 %collective-permute-done.8 = f32[832,384]{1,0:T(8,128)S(1)} collective-permute-done((f32[832,384]{1,0:T(8,128)S(1)}, f32[832,384]{1,0:T(8,128)S(1)}, u32[]{:S(2)}, u32[]{:S(2)}) %collective-permute-start.8) | collective-permute-done | bytes 1277984 | tf_op jit(solution)/shard_map/V1/ppermute | solution.py:649
  67.0 2.8 %shard_map.322 = (f32[704,384]{1,0:T(8,128)S(1)}, f32[704,384]{1,0:T(8,128)S(1)}, f32[864,384]{1,0:T(8,128)S(1)}, f32[832,384]{1,0:T(8,128)S(1)}) custom-call(s32[198]{0:T(256)S(1)} %bitcast.16, bf16[512,768]{1,0:T(8,128)(2,1)S(1)} %copy-done.2, bf16[512,384]{1,0:T(8,128)(2,1)S(1)} %copy-done.19, bf16[512,1152]{1,0:T(8,128)(2,1)S(1)} %get-tuple-element.158.grads, ...), custom_call_target="tpu_custom_call" | custom-call | flops 1 | bytes 1 | tf_op jit(solution)/shard_map/pallas_call | solution.py:143
  69.8 1.8 collective-permute-start.19
  72.2 12.0 %collective-permute-done.10 = f32[416,384]{1,0:T(8,128)S(1)} collective-permute-done((f32[416,384]{1,0:T(8,128)S(1)}, f32[416,384]{1,0:T(8,128)S(1)}, u32[]{:S(2)}, u32[]{:S(2)}) %collective-permute-start.10) | collective-permute-done | bytes 639008 | tf_op jit(solution)/shard_map/V2/ppermute | solution.py:649
  86.9 3.7 %collective-permute-start.14 = (f32[192,384]{1,0:T(8,128)S(1)}, f32[192,384]{1,0:T(8,128)S(1)}, u32[]{:S(2)}, u32[]{:S(2)}) collective-permute-start(f32[192,384]{1,0:T(8,128)S(1)} %fusion.2), channel_id=1, source_target_pairs={{0,24},{1,25},{2,26},{3,27},{4,28},{5,29},{6,30},{7,31},{8,16},{9,... | collective-permute-start | bytes 884744 | tf_op jit(solution)/shard_map/E4/ppermute | solution.py:649
  90.6 4.2 %collective-permute-done.13 = f32[208,384]{1,0:T(8,128)S(1)} collective-permute-done((f32[208,384]{1,0:T(8,128)S(1)}, f32[208,384]{1,0:T(8,128)S(1)}, u32[]{:S(2)}, u32[]{:S(2)}) %collective-permute-start.13) | collective-permute-done | bytes 319520 | tf_op jit(solution)/shard_map/V3/ppermute | solution.py:649
  94.8 2.7 %collective-permute-start.17 = (f32[192,384]{1,0:T(8,128)S(1)}, f32[192,384]{1,0:T(8,128)S(1)}, u32[]{:S(2)}, u32[]{:S(2)}) collective-permute-start(f32[192,384]{1,0:T(8,128)S(1)} %slice_add_fusion.17), channel_id=1, source_target_pairs={{0,4},{1,3},{2,6},{3,1},{4,0},{5,7},{6,2},{7,5},{8,12},{9,11},{10,... | collective-permute-start | bytes 884744 | tf_op jit(solution)/shard_map/D3/ppermute | solution.py:649
  97.6 4.9 %collective-permute-done.14 = f32[192,384]{1,0:T(8,128)S(1)} collective-permute-done((f32[192,384]{1,0:T(8,128)S(1)}, f32[192,384]{1,0:T(8,128)S(1)}, u32[]{:S(2)}, u32[]{:S(2)}) %collective-permute-start.14) | collective-permute-done | bytes 294944 | tf_op jit(solution)/shard_map/E4/ppermute | solution.py:649
  102.5 2.2 collective-permute-start.18
  104.7 3.5 %collective-permute-start.16 = (f32[192,384]{1,0:T(8,128)S(1)}, f32[192,384]{1,0:T(8,128)S(1)}, u32[]{:S(2)}, u32[]{:S(2)}) collective-permute-start(f32[192,384]{1,0:T(8,128)S(1)} %add.164), channel_id=1, source_target_pairs={{0,8},{1,9},{2,10},{3,11},{4,12},{5,13},{6,14},{7,15},{8,0},{9,1},... | collective-permute-start | bytes 884744 | tf_op jit(solution)/shard_map/E5/ppermute | solution.py:649
  108.3 3.2 %collective-permute-done.15 = f32[704,384]{1,0:T(8,128)S(1)} collective-permute-done((f32[704,384]{1,0:T(8,128)S(1)}, f32[704,384]{1,0:T(8,128)S(1)}, u32[]{:S(2)}, u32[]{:S(2)}) %collective-permute-start.15) | collective-permute-done | bytes 1081376 | tf_op jit(solution)/shard_map/R1/ppermute | solution.py:649
  112.9 3.9 %collective-permute-done.16 = f32[192,384]{1,0:T(8,128)S(1)} collective-permute-done((f32[192,384]{1,0:T(8,128)S(1)}, f32[192,384]{1,0:T(8,128)S(1)}, u32[]{:S(2)}, u32[]{:S(2)}) %collective-permute-start.16) | collective-permute-done | bytes 294944 | tf_op jit(solution)/shard_map/E5/ppermute | solution.py:649
  121.6 5.8 %collective-permute-done.20 = f32[352,384]{1,0:T(8,128)} collective-permute-done((f32[352,384]{1,0:T(8,128)}, f32[352,384]{1,0:T(8,128)}, u32[]{:S(2)}, u32[]{:S(2)}) %collective-permute-start.20) | collective-permute-done | bytes 540704 | tf_op jit(solution)/shard_map/R2/ppermute | solution.py:649
  133.7 2.4 collective-permute-done.22
  139.1 3.4 %collective-permute-start.28 = (f32[176,384]{1,0:T(8,128)S(1)}, f32[176,384]{1,0:T(8,128)S(1)}, u32[]{:S(2)}, u32[]{:S(2)}) collective-permute-start(f32[176,384]{1,0:T(8,128)S(1)} %fusion.4), channel_id=1, source_target_pairs={{0,24},{1,25},{2,26},{3,27},{4,28},{5,29},{6,30},{7,31},{8,16},{9,... | collective-permute-start | bytes 811016 | tf_op jit(solution)/shard_map/R4/ppermute | solution.py:649
  144.9 3.4 %collective-permute-done.26 = f32[352,384]{1,0:T(8,128)S(1)} collective-permute-done((f32[352,384]{1,0:T(8,128)S(1)}, f32[352,384]{1,0:T(8,128)S(1)}, u32[]{:S(2)}, u32[]{:S(2)}) %collective-permute-start.26) | collective-permute-done | bytes 540704 | tf_op jit(solution)/shard_map/U2/ppermute | solution.py:649
  148.3 2.0 collective-permute-start.30
  156.9 2.1 collective-permute-done.30
  161.4 5.3 %collective-permute-done.31 = f32[176,384]{1,0:T(8,128)S(1)} collective-permute-done((f32[176,384]{1,0:T(8,128)S(1)}, f32[176,384]{1,0:T(8,128)S(1)}, u32[]{:S(2)}, u32[]{:S(2)}) %collective-permute-start.31) | collective-permute-done | bytes 270368 | tf_op jit(solution)/shard_map/R5/ppermute | solution.py:649
  166.8 10.2 %collective-permute-start.34 = (f32[240,384]{1,0:T(8,128)S(1)}, f32[240,384]{1,0:T(8,128)S(1)}, u32[]{:S(2)}, u32[]{:S(2)}) collective-permute-start(f32[240,384]{1,0:T(8,128)S(1)} %pad_maximum_fusion.2), channel_id=1, source_target_pairs={{0,24},{1,25},{2,26},{3,27},{4,28},{5,29},{6,30},{7,31},{8,16},{9,... | collective-permute-start | bytes 1105928 | tf_op jit(solution)/shard_map/S4/ppermute | solution.py:649
  178.1 2.4 collective-permute-start.37
  180.6 2.8 %collective-permute-done.34 = f32[240,384]{1,0:T(8,128)S(1)} collective-permute-done((f32[240,384]{1,0:T(8,128)S(1)}, f32[240,384]{1,0:T(8,128)S(1)}, u32[]{:S(2)}, u32[]{:S(2)}) %collective-permute-start.34) | collective-permute-done | bytes 368672 | tf_op jit(solution)/shard_map/S4/ppermute | solution.py:649
  183.4 4.3 %collective-permute-start.38 = (f32[176,384]{1,0:T(8,128)S(1)}, f32[176,384]{1,0:T(8,128)S(1)}, u32[]{:S(2)}, u32[]{:S(2)}) collective-permute-start(f32[176,384]{1,0:T(8,128)S(1)} %fusion.3), channel_id=1, source_target_pairs={{0,24},{1,25},{2,26},{3,27},{4,28},{5,29},{6,30},{7,31},{8,16},{9,... | collective-permute-start | bytes 811016 | tf_op jit(solution)/shard_map/U4/ppermute | solution.py:649
  187.9 2.1 shard_map.323.rest_0_
  190.0 2.7 %collective-permute-start.39 = (f32[208,384]{1,0:T(8,128)S(1)}, f32[208,384]{1,0:T(8,128)S(1)}, u32[]{:S(2)}, u32[]{:S(2)}) collective-permute-start(f32[208,384]{1,0:T(8,128)S(1)} %slice.352), channel_id=1, source_target_pairs={{0,8},{1,9},{2,10},{3,11},{4,12},{5,13},{6,14},{7,15},{8,0},{9,1},... | collective-permute-start | bytes 958472 | tf_op jit(solution)/shard_map/S5/ppermute | solution.py:649
  194.0 3.1 %collective-permute-done.38 = f32[176,384]{1,0:T(8,128)S(1)} collective-permute-done((f32[176,384]{1,0:T(8,128)S(1)}, f32[176,384]{1,0:T(8,128)S(1)}, u32[]{:S(2)}, u32[]{:S(2)}) %collective-permute-start.38) | collective-permute-done | bytes 270368 | tf_op jit(solution)/shard_map/U4/ppermute | solution.py:649
  197.2 4.3 %collective-permute-done.39 = f32[208,384]{1,0:T(8,128)S(1)} collective-permute-done((f32[208,384]{1,0:T(8,128)S(1)}, f32[208,384]{1,0:T(8,128)S(1)}, u32[]{:S(2)}, u32[]{:S(2)}) %collective-permute-start.39) | collective-permute-done | bytes 319520 | tf_op jit(solution)/shard_map/S5/ppermute | solution.py:649
  203.3 2.0 shard_map.324.rest_0_
  205.4 3.6 %collective-permute-done.42 = f32[176,384]{1,0:T(8,128)S(1)} collective-permute-done((f32[176,384]{1,0:T(8,128)S(1)}, f32[176,384]{1,0:T(8,128)S(1)}, u32[]{:S(2)}, u32[]{:S(2)}) %collective-permute-start.42) | collective-permute-done | bytes 270368 | tf_op jit(solution)/shard_map/U5/ppermute | solution.py:649
  209.0 2.3 collective-permute-start.45
  211.4 6.1 %collective-permute-done.43 = f32[416,384]{1,0:T(8,128)S(1)} collective-permute-done((f32[416,384]{1,0:T(8,128)S(1)}, f32[416,384]{1,0:T(8,128)S(1)}, u32[]{:S(2)}, u32[]{:S(2)}) %collective-permute-start.43) | collective-permute-done | bytes 639008 | tf_op jit(solution)/shard_map/S6/ppermute | solution.py:649
  220.0 1.9 collective-permute-done.44.far
  221.9 1.9 shard_map.325
  223.9 5.1 %collective-permute-done.45 = f32[352,384]{1,0:T(8,128)S(1)} collective-permute-done((f32[352,384]{1,0:T(8,128)S(1)}, f32[352,384]{1,0:T(8,128)S(1)}, u32[]{:S(2)}, u32[]{:S(2)}) %collective-permute-start.45) | collective-permute-done | bytes 540704 | tf_op jit(solution)/shard_map/U6/ppermute | solution.py:649
  230.5 5.2 %collective-permute-done.46.far = f32[832,384]{1,0:T(8,128)S(1)} collective-permute-done((f32[832,384]{1,0:T(8,128)S(1)}, f32[832,384]{1,0:T(8,128)S(1)}, u32[]{:S(2)}, u32[]{:S(2)}) %collective-permute-start.46) | collective-permute-done | bytes 1277984 | tf_op jit(solution)/shard_map/S7/ppermute | solution.py:649
  235.6 2.1 shard_map.326
  237.7 2.0 shard_map.327
  241.6 5.6 %collective-permute-done.48.far = f32[704,384]{1,0:T(8,128)S(1)} collective-permute-done((f32[704,384]{1,0:T(8,128)S(1)}, f32[704,384]{1,0:T(8,128)S(1)}, u32[]{:S(2)}, u32[]{:S(2)}) %collective-permute-start.48) | collective-permute-done | bytes 1081376 | tf_op jit(solution)/shard_map/U7/ppermute | solution.py:649
  247.2 1.9 shard_map.328
  (197 shorter events, 56.3 us)
Async XLA Ops:
  9.2 3.6 %collective-permute-start = (f32[512,768]{1,0:T(8,128)S(1)}, f32[512,768]{1,0:T(8,128)S(1)}, u32[]{:S(2)}, u32[]{:S(2)}) collective-permute-start(f32[512,768]{1,0:T(8,128)S(1)} %get-tuple-element.119.refs_1_), channel_id=1, source_target_pairs={{0,1},{1,0},{2,3},{3,2},{4,5},{5,4},{6,7},{7,6},{8,9},{9,8},{10,11... | collective-permute-start | bytes 4718600 | tf_op jit(solution)/shard_map/ppermute | solution.py:642
  19.3 3.8 %collective-permute-start.1 = (f32[512,768]{1,0:T(8,128)}, f32[512,768]{1,0:T(8,128)}, u32[]{:S(2)}, u32[]{:S(2)}) collective-permute-start(f32[512,768]{1,0:T(8,128)} %get-tuple-element.121.refs_2_), channel_id=1, source_target_pairs={{0,1},{1,0},{2,3},{3,2},{4,5},{5,4},{6,7},{7,6},{8,9},{9,8},{10,11... | collective-permute-start | bytes 4718600 | tf_op jit(solution)/shard_map/ppermute | solution.py:642
  29.4 28.7 %collective-permute-start.6 = (f32[768,384]{1,0:T(8,128)S(1)}, f32[768,384]{1,0:T(8,128)S(1)}, u32[]{:S(2)}, u32[]{:S(2)}) collective-permute-start(f32[768,384]{1,0:T(8,128)S(1)} %get-tuple-element.127), channel_id=1, source_target_pairs={{0,2},{1,5},{2,0},{3,7},{4,6},{5,1},{6,4},{7,3},{8,10},{9,13},{10,... | collective-permute-start | bytes 3538952 | tf_op jit(solution)/shard_map/E1/ppermute | solution.py:649
  32.5 27.8 %collective-permute-start.7 = (f32[768,384]{1,0:T(8,128)S(1)}, f32[768,384]{1,0:T(8,128)S(1)}, u32[]{:S(2)}, u32[]{:S(2)}) collective-permute-start(f32[768,384]{1,0:T(8,128)S(1)} %get-tuple-element.126), channel_id=1, source_target_pairs={{0,8},{1,9},{2,10},{3,11},{4,12},{5,13},{6,14},{7,15},{8,0},{9,1},... | collective-permute-start | bytes 3538952 | tf_op jit(solution)/shard_map/D1/ppermute | solution.py:649
  45.3 1.7 collective-permute-start.2
  45.3 2.3 collective-permute-start.3
  45.8 19.3 %collective-permute-start.8 = (f32[832,384]{1,0:T(8,128)S(1)}, f32[832,384]{1,0:T(8,128)S(1)}, u32[]{:S(2)}, u32[]{:S(2)}) collective-permute-start(f32[832,384]{1,0:T(8,128)S(1)} %get-tuple-element.136), channel_id=1, source_target_pairs={{0,2},{1,5},{2,0},{3,7},{4,6},{5,1},{6,4},{7,3},{8,10},{9,13},{10,... | collective-permute-start | bytes 3833864 | tf_op jit(solution)/shard_map/V1/ppermute | solution.py:649
  47.0 1.7 collective-permute-start.4
  58.1 13.5 %collective-permute-start.9 = (f32[384,384]{1,0:T(8,128)S(1)}, f32[384,384]{1,0:T(8,128)S(1)}, u32[]{:S(2)}, u32[]{:S(2)}) collective-permute-start(f32[384,384]{1,0:T(8,128)S(1)} %slice_add_fusion.3), channel_id=1, source_target_pairs={{0,4},{1,3},{2,6},{3,1},{4,0},{5,7},{6,2},{7,5},{8,12},{9,11},{10,... | collective-permute-start | bytes 1769480 | tf_op jit(solution)/shard_map/E2/ppermute | solution.py:649
  65.2 19.0 %collective-permute-start.10 = (f32[416,384]{1,0:T(8,128)S(1)}, f32[416,384]{1,0:T(8,128)S(1)}, u32[]{:S(2)}, u32[]{:S(2)}) collective-permute-start(f32[416,384]{1,0:T(8,128)S(1)} %slice_add_fusion.1), channel_id=1, source_target_pairs={{0,4},{1,3},{2,6},{3,1},{4,0},{5,7},{6,2},{7,5},{8,12},{9,11},{10,... | collective-permute-start | bytes 1916936 | tf_op jit(solution)/shard_map/V2/ppermute | solution.py:649
  66.8 20.1 %collective-permute-start.12 = (f32[384,384]{1,0:T(8,128)S(1)}, f32[384,384]{1,0:T(8,128)S(1)}, u32[]{:S(2)}, u32[]{:S(2)}) collective-permute-start(f32[384,384]{1,0:T(8,128)S(1)} %slice_add_fusion.2), channel_id=1, source_target_pairs={{0,2},{1,5},{2,0},{3,7},{4,6},{5,1},{6,4},{7,3},{8,10},{9,13},{10,... | collective-permute-start | bytes 1769480 | tf_op jit(solution)/shard_map/D2/ppermute | solution.py:649
  69.8 34.9 %collective-permute-start.19 = (f32[864,384]{1,0:T(8,128)S(1)}, f32[864,384]{1,0:T(8,128)S(1)}, u32[]{:S(2)}, u32[]{:S(2)}) collective-permute-start(f32[864,384]{1,0:T(8,128)S(1)} %get-tuple-element.166), channel_id=1, source_target_pairs={{0,2},{1,5},{2,0},{3,7},{4,6},{5,1},{6,4},{7,3},{8,10},{9,13},{10,... | collective-permute-start | bytes 3981320 | tf_op jit(solution)/shard_map/S1/ppermute | solution.py:649
  71.7 14.7 %collective-permute-start.11 = (f32[192,384]{1,0:T(8,128)S(1)}, f32[192,384]{1,0:T(8,128)S(1)}, u32[]{:S(2)}, u32[]{:S(2)}) collective-permute-start(f32[192,384]{1,0:T(8,128)S(1)} %slice_add_fusion.21), channel_id=1, source_target_pairs={{0,8},{1,9},{2,10},{3,11},{4,12},{5,13},{6,14},{7,15},{8,0},{9,1},... | collective-permute-start | bytes 884744 | tf_op jit(solution)/shard_map/E3/ppermute | solution.py:649
  84.3 27.2 %collective-permute-start.15 = (f32[704,384]{1,0:T(8,128)S(1)}, f32[704,384]{1,0:T(8,128)S(1)}, u32[]{:S(2)}, u32[]{:S(2)}) collective-permute-start(f32[704,384]{1,0:T(8,128)S(1)} %get-tuple-element.170), channel_id=1, source_target_pairs={{0,2},{1,5},{2,0},{3,7},{4,6},{5,1},{6,4},{7,3},{8,10},{9,13},{10,... | collective-permute-start | bytes 3244040 | tf_op jit(solution)/shard_map/R1/ppermute | solution.py:649
  85.8 43.8 %collective-permute-start.21 = (f32[704,384]{1,0:T(8,128)}, f32[704,384]{1,0:T(8,128)}, u32[]{:S(2)}, u32[]{:S(2)}) collective-permute-start(f32[704,384]{1,0:T(8,128)} %get-tuple-element.167), channel_id=1, source_target_pairs={{0,2},{1,5},{2,0},{3,7},{4,6},{5,1},{6,4},{7,3},{8,10},{9,13},{10,... | collective-permute-start | bytes 3244040 | tf_op jit(solution)/shard_map/U1/ppermute | solution.py:649
  86.4 8.4 %collective-permute-start.13 = (f32[208,384]{1,0:T(8,128)S(1)}, f32[208,384]{1,0:T(8,128)S(1)}, u32[]{:S(2)}, u32[]{:S(2)}) collective-permute-start(f32[208,384]{1,0:T(8,128)S(1)} %slice_add_fusion.13), channel_id=1, source_target_pairs={{0,8},{1,9},{2,10},{3,11},{4,12},{5,13},{6,14},{7,15},{8,0},{9,1},... | collective-permute-start | bytes 958472 | tf_op jit(solution)/shard_map/V3/ppermute | solution.py:649
  86.9 15.6 %collective-permute-start.14 = (f32[192,384]{1,0:T(8,128)S(1)}, f32[192,384]{1,0:T(8,128)S(1)}, u32[]{:S(2)}, u32[]{:S(2)}) collective-permute-start(f32[192,384]{1,0:T(8,128)S(1)} %fusion.2), channel_id=1, source_target_pairs={{0,24},{1,25},{2,26},{3,27},{4,28},{5,29},{6,30},{7,31},{8,16},{9,... | collective-permute-start | bytes 884744 | tf_op jit(solution)/shard_map/E4/ppermute | solution.py:649
  94.8 22.1 %collective-permute-start.17 = (f32[192,384]{1,0:T(8,128)S(1)}, f32[192,384]{1,0:T(8,128)S(1)}, u32[]{:S(2)}, u32[]{:S(2)}) collective-permute-start(f32[192,384]{1,0:T(8,128)S(1)} %slice_add_fusion.17), channel_id=1, source_target_pairs={{0,4},{1,3},{2,6},{3,1},{4,0},{5,7},{6,2},{7,5},{8,12},{9,11},{10,... | collective-permute-start | bytes 884744 | tf_op jit(solution)/shard_map/D3/ppermute | solution.py:649
  102.5 14.5 %collective-permute-start.18 = (f32[208,384]{1,0:T(8,128)S(1)}, f32[208,384]{1,0:T(8,128)S(1)}, u32[]{:S(2)}, u32[]{:S(2)}) collective-permute-start(f32[208,384]{1,0:T(8,128)S(1)} %fusion), channel_id=1, source_target_pairs={{0,24},{1,25},{2,26},{3,27},{4,28},{5,29},{6,30},{7,31},{8,16},{9,... | collective-permute-start | bytes 958472 | tf_op jit(solution)/shard_map/V4/ppermute | solution.py:649
  104.7 12.1 %collective-permute-start.16 = (f32[192,384]{1,0:T(8,128)S(1)}, f32[192,384]{1,0:T(8,128)S(1)}, u32[]{:S(2)}, u32[]{:S(2)}) collective-permute-start(f32[192,384]{1,0:T(8,128)S(1)} %add.164), channel_id=1, source_target_pairs={{0,8},{1,9},{2,10},{3,11},{4,12},{5,13},{6,14},{7,15},{8,0},{9,1},... | collective-permute-start | bytes 884744 | tf_op jit(solution)/shard_map/E5/ppermute | solution.py:649
  112.5 14.9 %collective-permute-start.20 = (f32[352,384]{1,0:T(8,128)}, f32[352,384]{1,0:T(8,128)}, u32[]{:S(2)}, u32[]{:S(2)}) collective-permute-start(f32[352,384]{1,0:T(8,128)} %slice_add_fusion.5), channel_id=1, source_target_pairs={{0,8},{1,9},{2,10},{3,11},{4,12},{5,13},{6,14},{7,15},{8,0},{9,1},... | collective-permute-start | bytes 1622024 | tf_op jit(solution)/shard_map/R2/ppermute | solution.py:649
  118.8 13.8 %collective-permute-start.25 = (f32[448,384]{1,0:T(8,128)}, f32[448,384]{1,0:T(8,128)}, u32[]{:S(2)}, u32[]{:S(2)}) collective-permute-start(f32[448,384]{1,0:T(8,128)} %pad_maximum_fusion), channel_id=1, source_target_pairs={{0,4},{1,3},{2,6},{3,1},{4,0},{5,7},{6,2},{7,5},{8,12},{9,11},{10,... | collective-permute-start | bytes 2064392 | tf_op jit(solution)/shard_map/S2/ppermute | solution.py:649
  121.5 68.5 %collective-permute-start.36 = (f32[512,768]{1,0:T(8,128)S(1)}, f32[512,768]{1,0:T(8,128)S(1)}, u32[]{:S(2)}, u32[]{:S(2)}) collective-permute-start(f32[512,768]{1,0:T(8,128)S(1)} %shard_map.321), channel_id=1, source_target_pairs={{0,1},{1,0},{2,3},{3,2},{4,5},{5,4},{6,7},{7,6},{8,9},{9,8},{10,11... | collective-permute-start | bytes 4718600 | tf_op jit(solution)/shard_map/ppermute | solution.py:642
  121.5 17.6 %collective-permute-start.23 = (f32[192,384]{1,0:T(8,128)S(1)}, f32[192,384]{1,0:T(8,128)S(1)}, u32[]{:S(2)}, u32[]{:S(2)}) collective-permute-start(f32[192,384]{1,0:T(8,128)S(1)} %fusion.1), channel_id=1, source_target_pairs={{0,24},{1,25},{2,26},{3,27},{4,28},{5,29},{6,30},{7,31},{8,16},{9,... | collective-permute-start | bytes 884744 | tf_op jit(solution)/shard_map/D4/ppermute | solution.py:649
  127.4 15.2 %collective-permute-start.24 = (f32[208,384]{1,0:T(8,128)}, f32[208,384]{1,0:T(8,128)S(1)}, u32[]{:S(2)}, u32[]{:S(2)}) collective-permute-start(f32[208,384]{1,0:T(8,128)} %add.169), channel_id=1, source_target_pairs={{0,8},{1,9},{2,10},{3,11},{4,12},{5,13},{6,14},{7,15},{8,0},{9,1},... | collective-permute-start | bytes 958472 | tf_op jit(solution)/shard_map/V5/ppermute | solution.py:649
  129.7 6.5 %collective-permute-start.22 = (f32[176,384]{1,0:T(8,128)S(1)}, f32[176,384]{1,0:T(8,128)S(1)}, u32[]{:S(2)}, u32[]{:S(2)}) collective-permute-start(f32[176,384]{1,0:T(8,128)S(1)} %slice_add_fusion.29), channel_id=1, source_target_pairs={{0,4},{1,3},{2,6},{3,1},{4,0},{5,7},{6,2},{7,5},{8,12},{9,11},{10,... | collective-permute-start | bytes 811016 | tf_op jit(solution)/shard_map/R3/ppermute | solution.py:649
  132.6 18.8 %collective-permute-start.27 = (f32[384,384]{1,0:T(8,128)S(1)}, f32[384,384]{1,0:T(8,128)S(1)}, u32[]{:S(2)}, u32[]{:S(2)}) collective-permute-start(f32[384,384]{1,0:T(8,128)S(1)} %constant_dynamic-update-slice_fusion), channel_id=1, source_target_pairs={{0,4},{1,3},{2,6},{3,1},{4,0},{5,7},{6,2},{7,5},{8,12},{9,11},{10,... | collective-permute-start | bytes 1769480 | tf_op jit(solution)/shard_map/E6/ppermute | solution.py:649
  136.2 12.1 %collective-permute-start.26 = (f32[352,384]{1,0:T(8,128)S(1)}, f32[352,384]{1,0:T(8,128)S(1)}, u32[]{:S(2)}, u32[]{:S(2)}) collective-permute-start(f32[352,384]{1,0:T(8,128)S(1)} %slice_add_fusion.4), channel_id=1, source_target_pairs={{0,4},{1,3},{2,6},{3,1},{4,0},{5,7},{6,2},{7,5},{8,12},{9,11},{10,... | collective-permute-start | bytes 1622024 | tf_op jit(solution)/shard_map/U2/ppermute | solution.py:649
  139.1 14.1 %collective-permute-start.28 = (f32[176,384]{1,0:T(8,128)S(1)}, f32[176,384]{1,0:T(8,128)S(1)}, u32[]{:S(2)}, u32[]{:S(2)}) collective-permute-start(f32[176,384]{1,0:T(8,128)S(1)} %fusion.4), channel_id=1, source_target_pairs={{0,24},{1,25},{2,26},{3,27},{4,28},{5,29},{6,30},{7,31},{8,16},{9,... | collective-permute-start | bytes 811016 | tf_op jit(solution)/shard_map/R4/ppermute | solution.py:649
  142.7 12.5 %collective-permute-start.29 = (f32[416,384]{1,0:T(8,128)S(1)}, f32[416,384]{1,0:T(8,128)S(1)}, u32[]{:S(2)}, u32[]{:S(2)}) collective-permute-start(f32[416,384]{1,0:T(8,128)S(1)} %constant_dynamic-update-slice_fusion.2), channel_id=1, source_target_pairs={{0,4},{1,3},{2,6},{3,1},{4,0},{5,7},{6,2},{7,5},{8,12},{9,11},{10,... | collective-permute-start | bytes 1916936 | tf_op jit(solution)/shard_map/V6/ppermute | solution.py:649
  148.3 10.7 %collective-permute-start.30 = (f32[240,384]{1,0:T(8,128)S(1)}, f32[240,384]{1,0:T(8,128)S(1)}, u32[]{:S(2)}, u32[]{:S(2)}) collective-permute-start(f32[240,384]{1,0:T(8,128)S(1)} %pad_maximum_fusion.1), channel_id=1, source_target_pairs={{0,8},{1,9},{2,10},{3,11},{4,12},{5,13},{6,14},{7,15},{8,0},{9,1},... | collective-permute-start | bytes 1105928 | tf_op jit(solution)/shard_map/S3/ppermute | solution.py:649
  151.4 26.7 %collective-permute-start.33 = (f32[192,384]{1,0:T(8,128)S(1)}, f32[192,384]{1,0:T(8,128)S(1)}, u32[]{:S(2)}, u32[]{:S(2)}) collective-permute-start(f32[192,384]{1,0:T(8,128)S(1)} %add.178), channel_id=1, source_target_pairs={{0,4},{1,3},{2,6},{3,1},{4,0},{5,7},{6,2},{7,5},{8,12},{9,11},{10,... | collective-permute-start | bytes 884744 | tf_op jit(solution)/shard_map/D5/ppermute | solution.py:649
  153.2 13.6 %collective-permute-start.32 = (f32[176,384]{1,0:T(8,128)S(1)}, f32[176,384]{1,0:T(8,128)S(1)}, u32[]{:S(2)}, u32[]{:S(2)}) collective-permute-start(f32[176,384]{1,0:T(8,128)S(1)} %slice_add_fusion.25), channel_id=1, source_target_pairs={{0,8},{1,9},{2,10},{3,11},{4,12},{5,13},{6,14},{7,15},{8,0},{9,1},... | collective-permute-start | bytes 811016 | tf_op jit(solution)/shard_map/U3/ppermute | solution.py:649
  155.2 11.6 %collective-permute-start.31 = (f32[176,384]{1,0:T(8,128)S(1)}, f32[176,384]{1,0:T(8,128)S(1)}, u32[]{:S(2)}, u32[]{:S(2)}) collective-permute-start(f32[176,384]{1,0:T(8,128)S(1)} %add.184), channel_id=1, source_target_pairs={{0,4},{1,3},{2,6},{3,1},{4,0},{5,7},{6,2},{7,5},{8,12},{9,11},{10,... | collective-permute-start | bytes 811016 | tf_op jit(solution)/shard_map/R5/ppermute | solution.py:649
  159.0 28.8 %collective-permute-start.35 = (f32[832,384]{1,0:T(8,128)S(1)}, f32[832,384]{1,0:T(8,128)S(1)}, u32[]{:S(2)}, u32[]{:S(2)}) collective-permute-start(f32[832,384]{1,0:T(8,128)S(1)} %constant_dynamic-update-slice_fusion.6.near), channel_id=1, source_target_pairs={{0,2},{1,5},{2,0},{3,7},{4,6},{5,1},{6,4},{7,3},{8,10},{9,13},{10,... | collective-permute-start | bytes 3833864 | tf_op jit(solution)/shard_map/V7/ppermute | solution.py:649
  166.8 36.6 %collective-permute-start.41 = (f32[768,384]{1,0:T(8,128)S(1)}, f32[768,384]{1,0:T(8,128)S(1)}, u32[]{:S(2)}, u32[]{:S(2)}) collective-permute-start(f32[768,384]{1,0:T(8,128)S(1)} %constant_dynamic-update-slice_fusion.4.near), channel_id=1, source_target_pairs={{0,2},{1,5},{2,0},{3,7},{4,6},{5,1},{6,4},{7,3},{8,10},{9,13},{10,... | collective-permute-start | bytes 3538952 | tf_op jit(solution)/shard_map/E7/ppermute | solution.py:649
  166.8 16.6 %collective-permute-start.34 = (f32[240,384]{1,0:T(8,128)S(1)}, f32[240,384]{1,0:T(8,128)S(1)}, u32[]{:S(2)}, u32[]{:S(2)}) collective-permute-start(f32[240,384]{1,0:T(8,128)S(1)} %pad_maximum_fusion.2), channel_id=1, source_target_pairs={{0,24},{1,25},{2,26},{3,27},{4,28},{5,29},{6,30},{7,31},{8,16},{9,... | collective-permute-start | bytes 1105928 | tf_op jit(solution)/shard_map/S4/ppermute | solution.py:649
  178.1 15.9 %collective-permute-start.37 = (f32[352,384]{1,0:T(8,128)S(1)}, f32[352,384]{1,0:T(8,128)S(1)}, u32[]{:S(2)}, u32[]{:S(2)}) collective-permute-start(f32[352,384]{1,0:T(8,128)S(1)} %constant_dynamic-update-slice_fusion.8), channel_id=1, source_target_pairs={{0,8},{1,9},{2,10},{3,11},{4,12},{5,13},{6,14},{7,15},{8,0},{9,1},... | collective-permute-start | bytes 1622024 | tf_op jit(solution)/shard_map/R6/ppermute | solution.py:649
  183.4 13.7 %collective-permute-start.38 = (f32[176,384]{1,0:T(8,128)S(1)}, f32[176,384]{1,0:T(8,128)S(1)}, u32[]{:S(2)}, u32[]{:S(2)}) collective-permute-start(f32[176,384]{1,0:T(8,128)S(1)} %fusion.3), channel_id=1, source_target_pairs={{0,24},{1,25},{2,26},{3,27},{4,28},{5,29},{6,30},{7,31},{8,16},{9,... | collective-permute-start | bytes 811016 | tf_op jit(solution)/shard_map/U4/ppermute | solution.py:649
  187.8 15.5 %collective-permute-start.40 = (f32[384,384]{1,0:T(8,128)S(1)}, f32[384,384]{1,0:T(8,128)S(1)}, u32[]{:S(2)}, u32[]{:S(2)}) collective-permute-start(f32[384,384]{1,0:T(8,128)S(1)} %constant_dynamic-update-slice_fusion.10), channel_id=1, source_target_pairs={{0,2},{1,5},{2,0},{3,7},{4,6},{5,1},{6,4},{7,3},{8,10},{9,13},{10,... | collective-permute-start | bytes 1769480 | tf_op jit(solution)/shard_map/D6/ppermute | solution.py:649
  190.0 11.5 %collective-permute-start.39 = (f32[208,384]{1,0:T(8,128)S(1)}, f32[208,384]{1,0:T(8,128)S(1)}, u32[]{:S(2)}, u32[]{:S(2)}) collective-permute-start(f32[208,384]{1,0:T(8,128)S(1)} %slice.352), channel_id=1, source_target_pairs={{0,8},{1,9},{2,10},{3,11},{4,12},{5,13},{6,14},{7,15},{8,0},{9,1},... | collective-permute-start | bytes 958472 | tf_op jit(solution)/shard_map/S5/ppermute | solution.py:649
  201.5 15.9 %collective-permute-start.43 = (f32[416,384]{1,0:T(8,128)S(1)}, f32[416,384]{1,0:T(8,128)S(1)}, u32[]{:S(2)}, u32[]{:S(2)}) collective-permute-start(f32[416,384]{1,0:T(8,128)S(1)} %constant_dynamic-update-slice_fusion.14), channel_id=1, source_target_pairs={{0,4},{1,3},{2,6},{3,1},{4,0},{5,7},{6,2},{7,5},{8,12},{9,11},{10,... | collective-permute-start | bytes 1916936 | tf_op jit(solution)/shard_map/S6/ppermute | solution.py:649
  201.6 7.4 %collective-permute-start.42 = (f32[176,384]{1,0:T(8,128)S(1)}, f32[176,384]{1,0:T(8,128)S(1)}, u32[]{:S(2)}, u32[]{:S(2)}) collective-permute-start(f32[176,384]{1,0:T(8,128)S(1)} %add.195), channel_id=1, source_target_pairs={{0,8},{1,9},{2,10},{3,11},{4,12},{5,13},{6,14},{7,15},{8,0},{9,1},... | collective-permute-start | bytes 811016 | tf_op jit(solution)/shard_map/U5/ppermute | solution.py:649
  203.2 18.7 %collective-permute-start.44 = (f32[704,384]{1,0:T(8,128)S(1)}, f32[704,384]{1,0:T(8,128)S(1)}, u32[]{:S(2)}, u32[]{:S(2)}) collective-permute-start(f32[704,384]{1,0:T(8,128)S(1)} %constant_dynamic-update-slice_fusion.12.near), channel_id=1, source_target_pairs={{0,2},{1,5},{2,0},{3,7},{4,6},{5,1},{6,4},{7,3},{8,10},{9,13},{10,... | collective-permute-start | bytes 3244040 | tf_op jit(solution)/shard_map/R7/ppermute | solution.py:649
  209.0 20.0 %collective-permute-start.45 = (f32[352,384]{1,0:T(8,128)S(1)}, f32[352,384]{1,0:T(8,128)S(1)}, u32[]{:S(2)}, u32[]{:S(2)}) collective-permute-start(f32[352,384]{1,0:T(8,128)S(1)} %constant_dynamic-update-slice_fusion.18), channel_id=1, source_target_pairs={{0,4},{1,3},{2,6},{3,1},{4,0},{5,7},{6,2},{7,5},{8,12},{9,11},{10,... | collective-permute-start | bytes 1622024 | tf_op jit(solution)/shard_map/U6/ppermute | solution.py:649
  217.5 18.1 %collective-permute-start.46 = (f32[832,384]{1,0:T(8,128)S(1)}, f32[832,384]{1,0:T(8,128)S(1)}, u32[]{:S(2)}, u32[]{:S(2)}) collective-permute-start(f32[832,384]{1,0:T(8,128)S(1)} %constant_dynamic-update-slice_fusion.20.near), channel_id=1, source_target_pairs={{0,2},{1,5},{2,0},{3,7},{4,6},{5,1},{6,4},{7,3},{8,10},{9,13},{10,... | collective-permute-start | bytes 3833864 | tf_op jit(solution)/shard_map/S7/ppermute | solution.py:649
  218.9 18.8 %collective-permute-start.47 = (f32[768,384]{1,0:T(8,128)S(1)}, f32[768,384]{1,0:T(8,128)S(1)}, u32[]{:S(2)}, u32[]{:S(2)}) collective-permute-start(f32[768,384]{1,0:T(8,128)S(1)} %constant_dynamic-update-slice_fusion.16.near), channel_id=1, source_target_pairs={{0,8},{1,9},{2,10},{3,11},{4,12},{5,13},{6,14},{7,15},{8,0},{9,1},... | collective-permute-start | bytes 3538952 | tf_op jit(solution)/shard_map/D7/ppermute | solution.py:649
  229.1 18.1 %collective-permute-start.48 = (f32[704,384]{1,0:T(8,128)S(1)}, f32[704,384]{1,0:T(8,128)S(1)}, u32[]{:S(2)}, u32[]{:S(2)}) collective-permute-start(f32[704,384]{1,0:T(8,128)S(1)} %constant_dynamic-update-slice_fusion.22.near), channel_id=1, source_target_pairs={{0,2},{1,5},{2,0},{3,7},{4,6},{5,1},{6,4},{7,3},{8,10},{9,13},{10,... | collective-permute-start | bytes 3244040 | tf_op jit(solution)/shard_map/U7/ppermute | solution.py:649
  (35 other events, 329.6 us)
